TPU v7x, 256 devices: a whole 4x4x8 slice. The times are simulated.
256 devices in a mesh: dom: 64 (over y, z_lo, x, core), rep: 4 (over z_hi).
Axes of the slice: x: 4, y: 4, z: 8 (z_hi: 4, z_lo: 2; z = z_hi * 2 + z_lo), core: 2. Of those that a mesh axis runs over, the one named last changes fastest.
Arguments:
- entities: float32 [16384, 512], P('dom'), may hold values from -1.5 to 1.5
- ent_accum: float32 [16384], P('dom'), may hold values from 0.5 to 20
- relations: float32 [8, 512, 512], P('rep'), may hold values from -0.25 to 0.25
- rel_accum: float32 [8, 512, 512], P('rep'), may hold values from 29.4912 to 294.912
- heads: int32 [3, 196608], P(None, ('dom', 'rep')), may hold values from 0 to 255
- tails: int32 [3, 196608], P(None, ('dom', 'rep')), may hold values from 0 to 255
- relation_ids: int32 [3, 196608], P(None, ('dom', 'rep')), may hold values from 0 to 1
- negatives: int32 [3, 65536], P(None, ('dom', 'rep')), may hold values from 0 to 255
Outputs:
- new_entities: float32 [16384, 512], P('dom')
- new_ent_accum: float32 [16384], P('dom')
- new_relations: float32 [8, 512, 512], P('rep')
- new_rel_accum: float32 [8, 512, 512], P('rep')
Inputs may be any that keep to these rules, and one draw needn't show every extreme that they name: `negatives`: rows within the named partition; some rows are named far more often than others.
All inputs are finite; a program needn't handle non-finite values.
Results may differ from a plain program's by a relative error of at most 0.0077.
Values may be sent and summed in bfloat16 or wider, within the bound.
No kernel may reach another device: no remote copies, remote signals or barrier semaphores. Data moves between devices by JAX's collectives and lax.ppermute only.
A program may use at most 64 MiB of HBM per device.

v0:
```python
import functools
import math

import jax
import jax.numpy as jnp
from jax import lax
from jax.experimental import pallas as pl
from jax.experimental.pallas import tpu as pltpu
from jax.sharding import PartitionSpec as P


NCAP = 4
ROUNDS = 3
LANES = 128
INDEX_LINES = 16
FAR = 4 << 20

negative_weight = 0.0625
entity_rate = 0.05
relation_rate = 0.02

BF = jnp.bfloat16
F32 = jnp.float32


class Late:
    def __init__(self, source, target, buffer, sem):
        self.copy = pltpu.make_async_copy(source, target, sem)
        self.buffer = buffer

    def ready(self):
        self.copy.wait()
        return self.buffer

    def send(self):
        self.copy.start()


def call(kernel, outs, *args, late=None, far=(), scratch=(), vmem=53500):
    late = late or {}
    shapes = []
    for i, (shape, dtype) in enumerate(outs):
        whole = shape
        if i in far:
            row = math.prod(shape[1:]) * jnp.dtype(dtype).itemsize
            whole = (max(shape[0], FAR // row),) + tuple(shape[1:])
        shapes.append(jax.ShapeDtypeStruct(whole, dtype))
    moved = sum(math.prod(shape) * jnp.dtype(dtype).itemsize for shape, dtype in outs)
    moved += sum((a.size if i not in late else a.size // a.shape[0] * late[i]) * a.dtype.itemsize for i, a in enumerate(args))
    near = pl.BlockSpec(memory_space=pltpu.VMEM)
    hbm = pl.BlockSpec(memory_space=pltpu.HBM)
    count = len(late) + len(far)
    buffers = [pltpu.VMEM((late[i],) + args[i].shape[1:], args[i].dtype) for i in late]
    buffers += [pltpu.VMEM(*outs[i]) for i in far]
    sems = [pltpu.SemaphoreType.DMA((count,))] if count else []

    def body(*refs):
        refs = list(refs)
        sem = refs.pop() if count else None
        bufs = refs[len(refs) - count :]
        refs = refs[: len(refs) - count]
        for b, i in enumerate(late):
            refs[i] = Late(refs[i].at[: late[i]], bufs[b], bufs[b], sem.at[b])
            refs[i].send()
        sent = []
        for b, i in enumerate(far, len(late)):
            out = refs[len(args) + i].at[: outs[i][0][0]]
            refs[len(args) + i] = Late(bufs[b], out, bufs[b], sem.at[b])
            sent.append(refs[len(args) + i])
        kernel(*refs)
        for item in sent:
            item.ready()

    return pl.pallas_call(
        body,
        out_shape=shapes,
        in_specs=[hbm if i in late else near for i in range(len(args))],
        out_specs=[hbm if i in far else near for i in range(len(outs))],
        scratch_shapes=list(scratch) + buffers + sems,
        compiler_params=pltpu.CompilerParams(vmem_limit_bytes=vmem << 10),
        cost_estimate=pl.CostEstimate(flops=0, bytes_accessed=moved, transcendentals=0),
    )(*args)


def nn(a, b):
    return jnp.dot(a, b, preferred_element_type=F32)


def nt(a, b):
    return lax.dot_general(a, b, (((1,), (1,)), ((), ())), preferred_element_type=F32)


def tn(a, b):
    return lax.dot_general(a, b, (((0,), (0,)), ((), ())), preferred_element_type=F32)


def iota(shape, dim):
    return lax.broadcasted_iota(jnp.int32, shape, dim)


def one_hot_rows(count, index):
    return (iota((count, index.shape[1]), 0) == index).astype(F32).astype(BF)


def all_ways(block, axes):
    return lax.all_to_all(block, axes, split_axis=0, concat_axis=0, tiled=True)


def from_behind(block, axis, distance):
    n = lax.axis_size(axis)
    return lax.ppermute(block, axis, [((i - distance) % n, i) for i in range(n)])


def fill_container(out_ref, sel_ref, ent_ref, idx_ref, rnd):
    rows, width = ent_ref.shape
    cuts = width // LANES
    sel_ref[...] = tn(one_hot_rows(rows, idx_ref[rnd : rnd + 1]), ent_ref[...]).astype(BF)
    slots = sel_ref.shape[0]
    block = out_ref.shape[0] // cuts
    line = iota((block, slots), 0)
    which = (line // NCAP) % cuts
    slot = line // (NCAP * cuts) * NCAP + line % NCAP - iota((block, slots), 1)

    @pl.loop(0, cuts)
    def _(i):
        first = i * (block // cuts)
        out = jnp.zeros((block, LANES), F32)
        for cs in range(cuts):
            perm = ((slot + first == 0) & (which == cs)).astype(F32).astype(BF)
            out = out + nn(perm, sel_ref[:, cs * LANES : (cs + 1) * LANES])
        out_ref[pl.ds(pl.multiple_of(i * block, block), block), :] = out.astype(BF)


def round_kernel(in_ref, out_ref):
    out_ref.buffer[...] = in_ref.ready()[...].astype(BF)
    out_ref.send()


def serve_kernel(ent_ref, idx_ref, out_ref, sel_ref):
    fill_container(out_ref, sel_ref, ent_ref, idx_ref, 0)


def tail_kernel(rnd, ent_ref, rel_ref, par_ref, head_ref, tail_ref, kind_ref, tq_ref, at_ref, n_ref, dtail_ref, pick_ref):
    rows = ent_ref.shape[0]
    kinds = rel_ref.buffer.shape[0]
    now = slice(rnd, rnd + 1)
    pick_ref[...] = one_hot_rows(kinds * rows, kind_ref[now] * rows + head_ref[now])
    tail = tail_ref[now]
    ones = jnp.ones((8, tail.shape[1]), F32).astype(BF)
    n = nt(ones, pick_ref[...])
    n_ref[...] = n
    rel = rel_ref.ready()

    @pl.loop(0, kinds)
    def _(t):
        cut = pl.ds(pl.multiple_of(t * rows, rows), rows)
        tq_ref[cut, :] = nn(ent_ref[...], rel[t]).astype(BF)

    block = rows // 2

    @pl.loop(0, 2)
    def _(i):
        cut = pl.ds(pl.multiple_of(i * block, block), block)
        pick_t = iota((block, tail.shape[1]), 0) + i * block == tail
        c = jnp.sum(pick_t.astype(F32), axis=1, keepdims=True)
        joint = nt(pick_t.astype(F32).astype(BF), pick_ref[...])
        prob = jax.nn.sigmoid(nt(par_ref[cut, :], tq_ref[...]))
        weight = (negative_weight * c) * n[:1]
        at = (weight * prob + joint * ((1.0 - negative_weight) * prob - 1.0)).astype(BF)
        at_ref[cut, :] = at
        dtail_ref[cut, :] = nn(at, tq_ref[...]).astype(BF)


def main_kernel(con_ref, tq_ref, n_ref, at_ref, par_ref, rel_ref, tail_ref, *refs):
    neg_ref, an_ref, sum_ref, cut_ref = refs[-4:]
    dneg_ref, g_ref = refs[0], refs[-5]
    out_refs = refs[1:-5]
    slots, width = neg_ref.shape
    cuts = width // LANES
    kinds = rel_ref.buffer.shape[0]
    rows = par_ref.shape[0]
    reps = cut_ref.shape[0]
    idx_ref = None
    if len(out_refs) > reps:
        idx_ref, out_refs = out_refs[0], out_refs[1:]
        dneg_ref, idx_ref = idx_ref, dneg_ref
    slot = iota((slots, con_ref.shape[0]), 0)
    row = iota((slots, con_ref.shape[0]), 1) - ((slot // NCAP) * (NCAP * cuts) + slot % NCAP)

    @pl.loop(0, cuts)
    def _(cs):
        perm = (row == cs * NCAP).astype(F32).astype(BF)
        cut = pl.ds(pl.multiple_of(cs * LANES, LANES), LANES)
        neg_ref[:, cut] = nn(perm, con_ref[...]).astype(BF)

    wide = dneg_ref.shape[1]
    block = slots // 2

    @pl.loop(0, 2)
    def _(i):
        cut = pl.ds(pl.multiple_of(i * block, block), block)
        prob = jax.nn.sigmoid(nt(neg_ref[cut, :], tq_ref[...]))
        an = (negative_weight * n_ref[:1] * prob).astype(BF)
        an_ref[cut, :] = an
        dneg = nn(an, tq_ref[...]).astype(BF)
        for cs in range(width // wide):
            start = pl.multiple_of(cs * slots + i * block, block)
            dneg_ref[pl.ds(start, block), :] = dneg[:, cs * wide : (cs + 1) * wide]

    rel = rel_ref.ready()
    sum_ref[...] = tail_ref[...].astype(F32)

    half = rows // 2

    @pl.loop(0, 2 * kinds)
    def _(i):
        cut = pl.ds(pl.multiple_of(i * half, half), half)
        g = (tn(at_ref[:, cut], par_ref[...]) + tn(an_ref[:, cut], neg_ref[...])).astype(BF)
        g_ref.buffer[cut, :] = g
        head = pl.ds(pl.multiple_of(i % 2 * half, half), half)
        sum_ref[head, :] += nt(g, rel[i // 2])

    g_ref.send()
    for cs in range(reps):
        cut_ref[cs] = sum_ref[:, cs * wide : (cs + 1) * wide].astype(BF)
    mine = lax.axis_index("rep")
    for s in range(reps):
        out_refs[s][:rows, :] = cut_ref[lax.rem(mine + s, reps)]
        if idx_ref is not None:
            out_refs[s][rows:, :] = idx_ref[...]


def rel_kernel(*refs):
    given_ref, kept_ref, ents_ref = refs[2 * ROUNDS :]
    rows, width = ents_ref.shape[1:]
    for r in range(ROUNDS):
        ents_ref[r] = refs[r].ready()[...].astype(BF)
    g_refs = [ref.ready() for ref in refs[ROUNDS : 2 * ROUNDS]]
    core = lax.rem(lax.axis_index("dom"), 2)
    block = width // 4

    def half(which, out_ref):
        cut = pl.ds(pl.multiple_of(which * rows, rows), rows)

        @pl.loop(0, 4)
        def _(i):
            part = pl.ds(pl.multiple_of(i * block, block), block)
            total = sum(tn(ents_ref[r, :, part], g_refs[r][cut, :]) for r in range(ROUNDS))
            out_ref[part, :] = total.astype(out_ref.dtype)

    half(core, kept_ref.buffer)
    kept_ref.send()
    half(1 - core, given_ref)


def pair_kernel(kept_ref, got_ref, out_ref):
    out_ref[...] = (kept_ref.ready()[...] + got_ref[...].astype(F32)).astype(BF)


def join_kernel(rnd, neg_ref, *refs):
    reps = (len(refs) - 1) // 2
    part_refs, idx_refs, out_refs = refs[:reps], refs[reps : 2 * reps], refs[2 * reps :]
    out_ref = out_refs[0]
    rows = out_ref.shape[1]
    slots = neg_ref.shape[0] // reps
    lines = slots // LANES
    mine = lax.axis_index("rep")
    total = part_refs[0][:rows, :].astype(F32)
    for part_ref in part_refs[1:]:
        total = total + part_ref[:rows, :].astype(F32)
    for s, idx_ref in enumerate(idx_refs):
        first = idx_ref.shape[0] - INDEX_LINES + rnd * lines
        for line in range(lines):
            start = lax.rem(mine + reps - s, reps) * slots + line * LANES
            index = idx_ref[first + line : first + line + 1, :].astype(F32).astype(jnp.int32)
            total = total + nn(one_hot_rows(rows, index), neg_ref[pl.ds(pl.multiple_of(start, LANES), LANES), :])
    out_ref[...] = jnp.broadcast_to(total.astype(BF)[None], out_ref.shape)


def update(grad_ref, ent_ref, acc_ref, new_ref):
    reps, _, wide = grad_ref.shape
    grads = [grad_ref[j].astype(F32) for j in range(reps)]
    square = sum(jnp.sum(g * g, axis=-1, keepdims=True) for g in grads)
    acc = acc_ref[...] + square / (reps * wide)
    scale = entity_rate / jnp.sqrt(acc)
    ent = ent_ref.ready()
    for j in range(reps):
        cut = slice(j * wide, (j + 1) * wide)
        new_ref[:, cut] = ent[:, cut] - scale * grads[j]
    return acc


def last_update_kernel(*refs):
    ent_ref, acc_ref, new_ref, new_acc_ref, grad_ref = refs[-5:]
    reps = grad_ref.shape[0]
    mine = lax.axis_index("rep")
    for s, part_ref in enumerate(refs[:-5]):
        grad_ref[lax.rem(mine + s, reps)] = part_ref[...]
    acc = update(grad_ref, ent_ref, acc_ref, new_ref)
    new_acc_ref[...] = jnp.broadcast_to(acc, (acc.shape[0], LANES)).T[:8]


def update_kernel(rnd, grad_ref, ent_ref, acc_ref, idx_ref, new_acc_ref, bf_ref, con_ref, new_ref, keep_ref, sel_ref):
    new_acc_ref[...] = update(grad_ref, ent_ref, acc_ref, new_ref.buffer)
    new_ref.send()
    bf_ref[...] = new_ref.buffer[...].astype(BF)
    keep_ref.buffer[...] = bf_ref[...]
    keep_ref.send()
    fill_container(con_ref, sel_ref, bf_ref, idx_ref, rnd + 1)


def total_kernel(parts_ref, out_ref):
    parts, piece, width = parts_ref.shape
    pairs = parts_ref[...].reshape(parts // 2, 2, piece, width)
    total = jnp.sum(pairs.astype(F32), axis=0).astype(BF).reshape(2 * piece, width)
    out_ref[...] = jnp.broadcast_to(total[None], out_ref.shape)


def step(entities, ent_accum, relations, rel_accum, heads, tails, relation_ids, negatives):
    rows, width = entities.shape
    parts = lax.axis_size("dom")
    reps = lax.axis_size("rep")
    kinds = relations.shape[0]
    slots = parts * NCAP
    wide = width // reps
    cuts = width // LANES
    everyone = ("rep", "dom")

    asked = negatives.reshape(ROUNDS, parts, NCAP).transpose(1, 0, 2).reshape(parts, ROUNDS * NCAP)
    asked = all_ways(asked, "dom").reshape(parts, ROUNDS, NCAP).transpose(1, 0, 2)
    own = asked.reshape(ROUNDS, slots)
    asked = asked.reshape(ROUNDS * slots // LANES, LANES)
    asked = jnp.pad(asked, ((0, INDEX_LINES - asked.shape[0]), (0, 0))).astype(BF)

    ent_bf = entities.astype(BF)
    accum = ent_accum.reshape(rows, 1)
    chosen = pltpu.VMEM((slots, width), BF)
    (con,) = call(serve_kernel, [((parts * cuts * NCAP, LANES), BF)], ent_bf, own, scratch=[chosen])
    ents, gs = [entities], []
    (rel_bf,) = call(round_kernel, [(relations.shape, BF)], relations, late={0: kinds}, far=(0,))
    for rnd in range(ROUNDS):
        offset = rnd + 1
        last = rnd == ROUNDS - 1
        partner = from_behind(ent_bf, "dom", -offset)
        con = all_ways(con.reshape(parts, cuts * NCAP, LANES), "dom").reshape(parts * cuts * NCAP, LANES)
        tq, at, n, dtail = call(
            functools.partial(tail_kernel, rnd),
            [((kinds * rows, width), BF), ((rows, kinds * rows), BF), ((8, kinds * rows), F32), ((rows, width), BF)],
            ent_bf,
            rel_bf,
            partner,
            heads,
            tails,
            relation_ids,
            late={1: kinds},
            scratch=[pltpu.VMEM((kinds * rows, heads.shape[1]), BF)],
        )
        dtail = from_behind(dtail, "dom", offset)
        lines = 0 if rnd else INDEX_LINES
        dneg, *dhead, g = call(
            main_kernel,
            [((reps * slots, wide), BF)] + [((rows + lines, wide), BF)] * reps + [((kinds * rows, width), BF)],
            con,
            tq,
            n,
            at,
            partner,
            rel_bf,
            dtail,
            *([] if rnd else [asked]),
            late={5: kinds},
            far=(1 + reps,),
            scratch=[
                pltpu.VMEM((slots, width), BF),
                pltpu.VMEM((slots, kinds * rows), BF),
                pltpu.VMEM((rows, width), F32),
                pltpu.VMEM((reps, rows, wide), BF),
            ],
        )
        dneg = all_ways(dneg.reshape(reps * parts, NCAP, wide), everyone).reshape(reps * slots, wide)
        gs.append(g)
        for s in range(1, reps):
            dhead[s] = from_behind(dhead[s], "rep", s)
        if rnd == 0:
            served = dhead
        (grads,) = call(
            functools.partial(join_kernel, rnd), [((1 if last else reps, rows, wide), BF)], dneg, *dhead, *served
        )
        if rnd == 0:
            served = [part[rows:] for part in dhead]
        if last:
            parts_of = [grads[0]]
            for s in range(1, reps):
                parts_of.append(from_behind(grads[0], "rep", -s))
        else:
            grads = all_ways(grads, "rep")
        if last:
            entities, accum = call(
                last_update_kernel,
                [((rows, width), F32), ((8, rows), F32)],
                *parts_of,
                entities,
                accum,
                late={reps: rows},
                scratch=[pltpu.VMEM((reps, rows, wide), BF)],
            )
        else:
            accum, ent_bf, con, entities, keep = call(
                functools.partial(update_kernel, rnd),
                [
                    ((rows, 1), F32),
                    ((rows, width), BF),
                    ((parts * cuts * NCAP, LANES), BF),
                    ((rows, width), F32),
                    ((rows, width), BF),
                ],
                grads,
                entities,
                accum,
                own,
                late={1: rows},
                far=(3, 4),
                scratch=[chosen],
            )
            ents.append(keep)
    pair = [(i ^ 1, i) for i in range(parts)]
    given, kept = call(
        rel_kernel,
        [((width, width), BF), ((width, width), F32)],
        *ents,
        *gs,
        late={i: rows if i < ROUNDS else kinds * rows for i in range(2 * ROUNDS)},
        far=(1,),
        scratch=[pltpu.VMEM((ROUNDS, rows, width), BF)],
    )
    got = lax.ppermute(given, "dom", pair)
    (drel,) = call(pair_kernel, [((width, width), BF)], kept, got, late={0: width})
    piece = width // parts
    drel = all_ways(drel.reshape(parts, piece, width), "dom")
    (total,) = call(total_kernel, [((parts, kinds * piece, width), BF)], drel)
    total = all_ways(total, "dom")
    total = total.reshape(parts, kinds, piece, width).transpose(1, 0, 2, 3).reshape(kinds, width, width)
    total = total.astype(F32)
    new_rel_accum = rel_accum + total * total
    new_relations = relations - relation_rate * total * lax.rsqrt(new_rel_accum)
    return (entities, accum[0], new_relations, new_rel_accum)


def solution(mesh):
    in_specs = (
        P("dom", None),
        P("dom"),
        P("rep", None, None),
        P("rep", None, None),
        P(None, ("dom", "rep")),
        P(None, ("dom", "rep")),
        P(None, ("dom", "rep")),
        P(None, ("dom", "rep")),
    )
    out_specs = (P("dom", None), P("dom"), P("rep", None, None), P("rep", None, None))
    return jax.shard_map(step, mesh=mesh, in_specs=in_specs, out_specs=out_specs, check_vma=False)
```

profile of v0, /device:TPU:1, one launch (start us, length us, event | category | flops | bytes accessed | tf_op | source)
XLA Modules:
  0.0 292.3 jit_solution(6790812495500414356)
XLA Ops:
  0.6 1.1 convert_element_type.10.refs_0_
  1.7 3.3 %collective-permute-start = (bf16[256,512]{1,0:T(8,128)(2,1)S(1)}, bf16[256,512]{1,0:T(8,128)(2,1)S(1)}, u32[]{:S(2)}, u32[]{:S(2)}) collective-permute-start(bf16[256,512]{1,0:T(8,128)(2,1)S(1)} %convert_element_type.10.refs_0_), channel_id=1, source_target_pairs={{4,0},{8,4},{12,8},{16,12},{20,16},{24,20},{28,24},{32,28},{36,32}... | collective-permute-start | bytes 786440 | tf_op jit(solution)/shard_map/ppermute | solution.py:111
  5.0 0.8 reshape.78
  6.0 15.5 %all_to_all.59 = s32[64,1,12]{2,1,0:T(1,128)S(1)} all-to-all(s32[64,1,12]{2,1,0:T(1,128)S(1)} %copy.21), channel_id=1, replica_groups=mesh['dom'=64,'rep'=4] {'dom'}, dimensions={0} | all-to-all | bytes 6144 | tf_op jit(solution)/shard_map/all_to_all | solution.py:106
  21.8 2.2 shard_map.111
  24.0 4.7 %all-to-all-start.1 = ((bf16[64,16,128]{2,1,0:T(8,128)(2,1)}), bf16[64,16,128]{2,1,0:T(8,128)(2,1)S(1)}, u32[]{:S(2)}, u32[]{:S(2)}) async-start(bf16[64,16,128]{2,1,0:T(8,128)(2,1)} %bitcast.2), calls=%async_computation.1 | async-start | bytes 524288 | tf_op jit(solution)/shard_map/all_to_all | solution.py:106
  28.7 2.7 shard_map.112.refs_1_.refs_5_
  31.5 3.4 %shard_map.113 = (bf16[512,512]{1,0:T(8,128)(2,1)S(1)}, bf16[256,512]{1,0:T(8,128)(2,1)S(1)}, f32[8,512]{1,0:T(8,128)S(1)}, bf16[256,512]{1,0:T(8,128)(2,1)S(1)}) custom-call(bf16[256,512]{1,0:T(8,128)(2,1)S(1)} %convert_element_type.10.refs_0_, bf16[8,512,512]{2,1,0:T(8,128)(2,1)} %shard_map.112.refs_1_.refs_5_, ...), custom_call_target="tpu_custom_call" | custom-call | bytes 2665472 | tf_op jit(solution)/shard_map/pallas_call | solution.py:74
  35.7 1.6 collective-permute-start.1
  37.6 1.0 all-to-all-done.1
  38.6 2.1 collective-permute-done.1.refs_6_
  40.7 6.5 %shard_map.114 = (bf16[1024,128]{1,0:T(8,128)(2,1)}, bf16[272,128]{1,0:T(8,128)(2,1)S(1)}, bf16[272,128]{1,0:T(8,128)(2,1)S(1)}, bf16[272,128]{1,0:T(8,128)(2,1)...) custom-call(bf16[1024,128]{1,0:T(8,128)(2,1)S(1)} %bitcast.39, bf16[512,512]{1,0:T(8,128)(2,1)} %copy-done.1, ...), custom_call_target="tpu_custom_call" | custom-call | bytes 3706880 | tf_op jit(solution)/shard_map/pallas_call | solution.py:74
  47.2 15.2 %all-to-all-start.2 = ((bf16[256,4,128]{2,1,0:T(4,128)(2,1)}), bf16[256,4,128]{2,1,0:T(4,128)(2,1)S(1)}, u32[]{:S(2)}, u32[]{:S(2)}) async-start(bf16[256,4,128]{2,1,0:T(4,128)(2,1)} %bitcast.4), calls=%async_computation.2 | async-start | bytes 524288 | tf_op jit(solution)/shard_map/all_to_all | solution.py:106
  62.4 2.7 collective-permute-start.2
  65.2 4.4 %collective-permute-start.3 = (bf16[272,128]{1,0:T(8,128)(2,1)S(1)}, bf16[272,128]{1,0:T(8,128)(2,1)S(1)}, u32[]{:S(2)}, u32[]{:S(2)}) collective-permute-start(bf16[272,128]{1,0:T(8,128)(2,1)S(1)} %get-tuple-element.55), channel_id=1, source_target_pairs={{2,0},{3,1},{0,2},{1,3},{6,4},{7,5},{4,6},{5,7},{10,8},{11,9},{8,1... | collective-permute-start | bytes 208904 | tf_op jit(solution)/shard_map/ppermute | solution.py:111
  69.5 2.8 collective-permute-start.4
  72.3 2.2 collective-permute-done.2.refs_2_.refs_6_
  74.5 4.9 %collective-permute-done.3.refs_3_.refs_7_ = bf16[272,128]{1,0:T(8,128)(2,1)S(1)} collective-permute-done((bf16[272,128]{1,0:T(8,128)(2,1)S(1)}, bf16[272,128]{1,0:T(8,128)(2,1)S(1)}, u32[]{:S(2)}, u32[]{:S(2)}) %collective-permute-start.3) | collective-permute-done | bytes 69664 | tf_op jit(solution)/shard_map/ppermute | solution.py:111
  79.4 1.0 shard_map.115
  80.4 3.4 %all-to-all-start.3 = ((bf16[4,256,128]{2,1,0:T(8,128)(2,1)}), bf16[4,256,128]{2,1,0:T(8,128)(2,1)S(1)}, u32[]{:S(2)}, u32[]{:S(2)}) async-start(bf16[4,256,128]{2,1,0:T(8,128)(2,1)} %shard_map.115), calls=%async_computation.3 | async-start | bytes 524288 | tf_op jit(solution)/shard_map/all_to_all | solution.py:106
  83.9 8.7 %all-to-all-done.3.refs_0_ = bf16[4,256,128]{2,1,0:T(8,128)(2,1)S(1)} async-done(((bf16[4,256,128]{2,1,0:T(8,128)(2,1)}), bf16[4,256,128]{2,1,0:T(8,128)(2,1)S(1)}, u32[]{:S(2)}, u32[]{:S(2)}) %all-to-all-start.3) | async-done | bytes 262176 | tf_op jit(solution)/shard_map/all_to_all | solution.py:106
  92.6 2.5 shard_map.116
  95.1 3.3 %collective-permute-start.5 = (bf16[256,512]{1,0:T(8,128)(2,1)S(1)}, bf16[256,512]{1,0:T(8,128)(2,1)S(1)}, u32[]{:S(2)}, u32[]{:S(2)}) collective-permute-start(bf16[256,512]{1,0:T(8,128)(2,1)S(1)} %get-tuple-element.58.refs_0_), channel_id=1, source_target_pairs={{8,0},{12,4},{16,8},{20,12},{24,16},{28,20},{32,24},{36,28},{40,32... | collective-permute-start | bytes 786440 | tf_op jit(solution)/shard_map/ppermute | solution.py:111
  98.5 8.0 %all-to-all-start.4 = ((bf16[64,16,128]{2,1,0:T(8,128)(2,1)}), bf16[64,16,128]{2,1,0:T(8,128)(2,1)S(1)}, u32[]{:S(2)}, u32[]{:S(2)}) async-start(bf16[64,16,128]{2,1,0:T(8,128)(2,1)} %bitcast.7), calls=%async_computation.4 | async-start | bytes 524288 | tf_op jit(solution)/shard_map/all_to_all | solution.py:106
  106.5 3.4 %shard_map.117 = (bf16[512,512]{1,0:T(8,128)(2,1)S(1)}, bf16[256,512]{1,0:T(8,128)(2,1)S(1)}, f32[8,512]{1,0:T(8,128)S(1)}, bf16[256,512]{1,0:T(8,128)(2,1)S(1)}) custom-call(bf16[256,512]{1,0:T(8,128)(2,1)S(1)} %get-tuple-element.58.refs_0_, bf16[8,512,512]{2,1,0:T(8,128)(2,1)} %shard_map.112.refs_1_.refs_5_, ...), custom_call_target="tpu_custom_call" | custom-call | bytes 2665472 | tf_op jit(solution)/shard_map/pallas_call | solution.py:74
  110.7 1.4 collective-permute-start.6
  112.1 4.3 %all-to-all-done.4 = bf16[64,16,128]{2,1,0:T(8,128)(2,1)S(1)} async-done(((bf16[64,16,128]{2,1,0:T(8,128)(2,1)}), bf16[64,16,128]{2,1,0:T(8,128)(2,1)S(1)}, u32[]{:S(2)}, u32[]{:S(2)}) %all-to-all-start.4) | async-done | bytes 262176 | tf_op jit(solution)/shard_map/all_to_all | solution.py:106
  116.4 6.4 %collective-permute-done.6.refs_6_ = bf16[256,512]{1,0:T(8,128)(2,1)S(1)} collective-permute-done((bf16[256,512]{1,0:T(8,128)(2,1)S(1)}, bf16[256,512]{1,0:T(8,128)(2,1)S(1)}, u32[]{:S(2)}, u32[]{:S(2)}) %collective-permute-start.6) | collective-permute-done | bytes 262176 | tf_op jit(solution)/shard_map/ppermute | solution.py:111
  122.9 6.5 %shard_map.118 = (bf16[1024,128]{1,0:T(8,128)(2,1)}, bf16[256,128]{1,0:T(8,128)(2,1)S(1)}, bf16[256,128]{1,0:T(8,128)(2,1)S(1)}, bf16[256,128]{1,0:T(8,128)(2,1)...) custom-call(bf16[1024,128]{1,0:T(8,128)(2,1)S(1)} %bitcast.42, bf16[512,512]{1,0:T(8,128)(2,1)} %copy-done.3, ...), custom_call_target="tpu_custom_call" | custom-call | bytes 3686400 | tf_op jit(solution)/shard_map/pallas_call | solution.py:74
  129.4 6.9 %all-to-all-start.5 = ((bf16[256,4,128]{2,1,0:T(4,128)(2,1)}), bf16[256,4,128]{2,1,0:T(4,128)(2,1)S(1)}, u32[]{:S(2)}, u32[]{:S(2)}) async-start(bf16[256,4,128]{2,1,0:T(4,128)(2,1)} %bitcast.9), calls=%async_computation.5 | async-start | bytes 524288 | tf_op jit(solution)/shard_map/all_to_all | solution.py:106
  136.3 2.7 collective-permute-start.7
  139.0 4.4 %collective-permute-start.8 = (bf16[256,128]{1,0:T(8,128)(2,1)S(1)}, bf16[256,128]{1,0:T(8,128)(2,1)S(1)}, u32[]{:S(2)}, u32[]{:S(2)}) collective-permute-start(bf16[256,128]{1,0:T(8,128)(2,1)S(1)} %get-tuple-element.66), channel_id=1, source_target_pairs={{2,0},{3,1},{0,2},{1,3},{6,4},{7,5},{4,6},{5,7},{10,8},{11,9},{8,1... | collective-permute-start | bytes 196616 | tf_op jit(solution)/shard_map/ppermute | solution.py:111
  143.4 2.8 collective-permute-start.9
  146.2 2.0 collective-permute-done.7.refs_2_
  148.2 4.7 %collective-permute-done.8.refs_3_ = bf16[256,128]{1,0:T(8,128)(2,1)S(1)} collective-permute-done((bf16[256,128]{1,0:T(8,128)(2,1)S(1)}, bf16[256,128]{1,0:T(8,128)(2,1)S(1)}, u32[]{:S(2)}, u32[]{:S(2)}) %collective-permute-start.8) | collective-permute-done | bytes 65568 | tf_op jit(solution)/shard_map/ppermute | solution.py:111
  153.2 12.1 %all_to_all.60.refs_0_ = bf16[4,256,128]{2,1,0:T(8,128)(2,1)S(1)} all-to-all(bf16[4,256,128]{2,1,0:T(8,128)(2,1)S(1)} %shard_map.119), channel_id=1, replica_groups=mesh['dom'=64,'rep'=4] {'rep'}, dimensions={0} | all-to-all | bytes 524288 | tf_op jit(solution)/shard_map/all_to_all | solution.py:106
  165.3 3.4 %shard_map.120 = (f32[256,1]{1,0:T(8,128)S(1)}, bf16[256,512]{1,0:T(8,128)(2,1)S(1)}, bf16[1024,128]{1,0:T(8,128)(2,1)}, f32[2048,512]{1,0:T(8,128)}, bf16[4096,512]{1,0:T(8,128)(2,1)}) custom-call(bf16[4,256,128]{2,1,0:T(8,128)(2,1)S(1)} %all_to_all.60.refs_0_, f32[2048,512]{1,0:T(8,128)} %get-tuple-element.68.refs_1_, ...), custom_call_target="tpu_custom_call" | custom-call | bytes 2102272 | tf_op jit(solution)/shard_map/pallas_call | solution.py:74
  168.7 7.0 %collective-permute-start.10 = (bf16[256,512]{1,0:T(8,128)(2,1)S(1)}, bf16[256,512]{1,0:T(8,128)(2,1)S(1)}, u32[]{:S(2)}, u32[]{:S(2)}) collective-permute-start(bf16[256,512]{1,0:T(8,128)(2,1)S(1)} %get-tuple-element.71.refs_0_), channel_id=1, source_target_pairs={{12,0},{16,4},{20,8},{24,12},{28,16},{32,20},{36,24},{40,28},{44,3... | collective-permute-start | bytes 786440 | tf_op jit(solution)/shard_map/ppermute | solution.py:111
  175.7 4.2 %all-to-all-start.7 = ((bf16[64,16,128]{2,1,0:T(8,128)(2,1)}), bf16[64,16,128]{2,1,0:T(8,128)(2,1)S(1)}, u32[]{:S(2)}, u32[]{:S(2)}) async-start(bf16[64,16,128]{2,1,0:T(8,128)(2,1)} %bitcast.11), calls=%async_computation.7 | async-start | bytes 524288 | tf_op jit(solution)/shard_map/all_to_all | solution.py:106
  179.9 3.4 %shard_map.121 = (bf16[512,512]{1,0:T(8,128)(2,1)S(1)}, bf16[256,512]{1,0:T(8,128)(2,1)S(1)}, f32[8,512]{1,0:T(8,128)S(1)}, bf16[256,512]{1,0:T(8,128)(2,1)S(1)}) custom-call(bf16[256,512]{1,0:T(8,128)(2,1)S(1)} %get-tuple-element.71.refs_0_, bf16[8,512,512]{2,1,0:T(8,128)(2,1)} %shard_map.112.refs_1_.refs_5_, ...), custom_call_target="tpu_custom_call" | custom-call | bytes 2665472 | tf_op jit(solution)/shard_map/pallas_call | solution.py:74
  184.1 2.8 collective-permute-start.11
  187.0 2.4 all-to-all-done.7
  189.4 7.6 %collective-permute-done.11.refs_6_ = bf16[256,512]{1,0:T(8,128)(2,1)S(1)} collective-permute-done((bf16[256,512]{1,0:T(8,128)(2,1)S(1)}, bf16[256,512]{1,0:T(8,128)(2,1)S(1)}, u32[]{:S(2)}, u32[]{:S(2)}) %collective-permute-start.11) | collective-permute-done | bytes 262176 | tf_op jit(solution)/shard_map/ppermute | solution.py:111
  197.0 6.5 %shard_map.122 = (bf16[1024,128]{1,0:T(8,128)(2,1)}, bf16[256,128]{1,0:T(8,128)(2,1)S(1)}, bf16[256,128]{1,0:T(8,128)(2,1)S(1)}, bf16[256,128]{1,0:T(8,128)(2,1)...) custom-call(bf16[1024,128]{1,0:T(8,128)(2,1)S(1)} %bitcast.41, bf16[512,512]{1,0:T(8,128)(2,1)} %copy-done.2, ...), custom_call_target="tpu_custom_call" | custom-call | bytes 3686400 | tf_op jit(solution)/shard_map/pallas_call | solution.py:74
  203.5 4.0 %shard_map.125 = (bf16[512,512]{1,0:T(8,128)(2,1)S(1)}, f32[2048,512]{1,0:T(8,128)}) custom-call(f32[256,512]{1,0:T(8,128)S(1)} %copy-done, bf16[4096,512]{1,0:T(8,128)(2,1)} %get-tuple-element.85.refs_1_, bf16[4096,512]{1,0:T(8,128)(2,1)} %get-tuple-element.86.refs_2_, bf16[4096,512]{1,0:T(8,128)(2,1)} %get-tuple-element.87.refs_3_, ...), custom_call_target="tpu_custom_call" | custom-call | bytes 4194304 | tf_op jit(solution)/shard_map/pallas_call | solution.py:74
  207.9 1.9 collective-permute-done.18.refs_1_
  209.8 1.4 shard_map.126
  211.1 16.9 %all_to_all.61.refs_0_ = bf16[64,8,512]{2,1,0:T(8,128)(2,1)S(1)} all-to-all(bf16[64,8,512]{2,1,0:T(8,128)(2,1)S(1)} %bitcast.38), channel_id=1, replica_groups=mesh['dom'=64,'rep'=4] {'dom'}, dimensions={0} | all-to-all | bytes 1048576 | tf_op jit(solution)/shard_map/all_to_all | solution.py:106
  228.1 5.5 %all-to-all-start.8 = ((bf16[256,4,128]{2,1,0:T(4,128)(2,1)}), bf16[256,4,128]{2,1,0:T(4,128)(2,1)S(1)}, u32[]{:S(2)}, u32[]{:S(2)}) async-start(bf16[256,4,128]{2,1,0:T(4,128)(2,1)} %bitcast.13), calls=%async_computation.8 | async-start | bytes 524288 | tf_op jit(solution)/shard_map/all_to_all | solution.py:106
  233.5 1.1 shard_map.127
  234.7 14.4 %all-to-all-done.8 = bf16[256,4,128]{2,1,0:T(4,128)(2,1)S(1)} async-done(((bf16[256,4,128]{2,1,0:T(4,128)(2,1)}), bf16[256,4,128]{2,1,0:T(4,128)(2,1)S(1)}, u32[]{:S(2)}, u32[]{:S(2)}) %all-to-all-start.8) | async-done | bytes 262176 | tf_op jit(solution)/shard_map/all_to_all | solution.py:106
  249.1 5.2 %all-to-all-start.10 = ((bf16[64,16,512]{2,1,0:T(8,128)(2,1)}), bf16[64,16,512]{2,1,0:T(8,128)(2,1)S(1)}, u32[]{:S(2)}, u32[]{:S(2)}) async-start(bf16[64,16,512]{2,1,0:T(8,128)(2,1)} %shard_map.127), calls=%async_computation.10 | async-start | bytes 2097152 | tf_op jit(solution)/shard_map/all_to_all | solution.py:106
  254.6 2.4 collective-permute-start.13
  257.0 1.3 collective-permute-start.14
  258.3 11.3 %collective-permute-done.12.refs_2_ = bf16[256,128]{1,0:T(8,128)(2,1)S(1)} collective-permute-done((bf16[256,128]{1,0:T(8,128)(2,1)S(1)}, bf16[256,128]{1,0:T(8,128)(2,1)S(1)}, u32[]{:S(2)}, u32[]{:S(2)}) %collective-permute-start.12) | collective-permute-done | bytes 65568 | tf_op jit(solution)/shard_map/ppermute | solution.py:111
  269.6 1.0 collective-permute-done.13.refs_3_
  270.9 3.7 %collective-permute-start.17 = (bf16[256,128]{1,0:T(8,128)(2,1)S(1)}, bf16[256,128]{1,0:T(8,128)(2,1)S(1)}, u32[]{:S(2)}, u32[]{:S(2)}) collective-permute-start(bf16[256,128]{1,0:T(8,128)(2,1)S(1)} %bitcast.45), channel_id=1, source_target_pairs={{3,0},{0,1},{1,2},{2,3},{7,4},{4,5},{5,6},{6,7},{11,8},{8,9},{9,10... | collective-permute-start | bytes 196616 | tf_op jit(solution)/shard_map/ppermute | solution.py:111
  274.7 1.7 collective-permute-start.16
  276.4 3.5 %collective-permute-start.15 = (bf16[256,128]{1,0:T(8,128)(2,1)S(1)}, bf16[256,128]{1,0:T(8,128)(2,1)S(1)}, u32[]{:S(2)}, u32[]{:S(2)}) collective-permute-start(bf16[256,128]{1,0:T(8,128)(2,1)S(1)} %bitcast.47), channel_id=1, source_target_pairs={{1,0},{2,1},{3,2},{0,3},{5,4},{6,5},{7,6},{4,7},{9,8},{10,9},{11,1... | collective-permute-start | bytes 196616 | tf_op jit(solution)/shard_map/ppermute | solution.py:111
  279.9 2.2 collective-permute-done.16.refs_2_
  282.1 2.5 collective-permute-done.15.refs_1_
  284.5 2.0 shard_map.124
  287.6 1.0 copy-done.7
  289.3 3.0 %fusion.2 = (f32[2,512,512]{2,1,0:T(8,128)}, f32[2,512,512]{2,1,0:T(8,128)}) fusion(f32[2,512,512]{2,1,0:T(8,128)S(1)} %copy-done.7, f32[2,64,8,512]{3,2,0,1:T(8,128)S(1)} %get-tuple-element.95, f32[2,512,512]{2,1,0:T(8,128)S(1)} %copy-done.8, f32[2,64,8,512]{3,2,0,1:T(8,128)S(1)} %get-tuple-element.94), kind=kLoop, calls=%fused_computation.6 | loop fusion | flops 1572864 | bytes 12582912 | tf_op jit(solution)/shard_map/sub | solution.py:445
  (51 shorter events, 6.2 us)
Async XLA Ops:
  1.7 29.7 %collective-permute-start = (bf16[256,512]{1,0:T(8,128)(2,1)S(1)}, bf16[256,512]{1,0:T(8,128)(2,1)S(1)}, u32[]{:S(2)}, u32[]{:S(2)}) collective-permute-start(bf16[256,512]{1,0:T(8,128)(2,1)S(1)} %convert_element_type.10.refs_0_), channel_id=1, source_target_pairs={{4,0},{8,4},{12,8},{16,12},{20,16},{24,20},{28,24},{32,28},{36,32}... | collective-permute-start | bytes 786440 | tf_op jit(solution)/shard_map/ppermute | solution.py:111
  24.0 14.6 %all-to-all-start.1 = ((bf16[64,16,128]{2,1,0:T(8,128)(2,1)}), bf16[64,16,128]{2,1,0:T(8,128)(2,1)S(1)}, u32[]{:S(2)}, u32[]{:S(2)}) async-start(bf16[64,16,128]{2,1,0:T(8,128)(2,1)} %bitcast.2), calls=%async_computation.1 | async-start | bytes 524288 | tf_op jit(solution)/shard_map/all_to_all | solution.py:106
  28.7 2.7 copy-start.4
  28.7 2.7 copy-start.5
  28.7 2.7 copy-start.6
  34.9 0.8 copy-start.1
  35.7 5.0 %collective-permute-start.1 = (bf16[256,512]{1,0:T(8,128)(2,1)S(1)}, bf16[256,512]{1,0:T(8,128)(2,1)S(1)}, u32[]{:S(2)}, u32[]{:S(2)}) collective-permute-start(bf16[256,512]{1,0:T(8,128)(2,1)S(1)} %get-tuple-element.51), channel_id=1, source_target_pairs={{252,0},{0,4},{4,8},{8,12},{12,16},{16,20},{20,24},{24,28},{28,32}... | collective-permute-start | bytes 786440 | tf_op jit(solution)/shard_map/ppermute | solution.py:111
  47.2 36.6 %copy-start.9 = (f32[256]{0:T(256)S(1)}, f32[256]{0:T(256)}, u32[]{:S(2)}) copy-start(f32[256]{0:T(256)} %param.9) | copy-start | bytes 3076
  47.2 45.4 %copy-start = (f32[256,512]{1,0:T(8,128)S(1)}, f32[256,512]{1,0:T(8,128)}, u32[]{:S(2)}) copy-start(f32[256,512]{1,0:T(8,128)} %refs_0_.3) | copy-start | bytes 1572868
  47.2 32.1 %all-to-all-start.2 = ((bf16[256,4,128]{2,1,0:T(4,128)(2,1)}), bf16[256,4,128]{2,1,0:T(4,128)(2,1)S(1)}, u32[]{:S(2)}, u32[]{:S(2)}) async-start(bf16[256,4,128]{2,1,0:T(4,128)(2,1)} %bitcast.4), calls=%async_computation.2 | async-start | bytes 524288 | tf_op jit(solution)/shard_map/all_to_all | solution.py:106
  62.4 12.0 %collective-permute-start.2 = (bf16[272,128]{1,0:T(8,128)(2,1)S(1)}, bf16[272,128]{1,0:T(8,128)(2,1)S(1)}, u32[]{:S(2)}, u32[]{:S(2)}) collective-permute-start(bf16[272,128]{1,0:T(8,128)(2,1)S(1)} %get-tuple-element.54), channel_id=1, source_target_pairs={{3,0},{0,1},{1,2},{2,3},{7,4},{4,5},{5,6},{6,7},{11,8},{8,9},{9,10... | collective-permute-start | bytes 208904 | tf_op jit(solution)/shard_map/ppermute | solution.py:111
  65.2 14.2 %collective-permute-start.3 = (bf16[272,128]{1,0:T(8,128)(2,1)S(1)}, bf16[272,128]{1,0:T(8,128)(2,1)S(1)}, u32[]{:S(2)}, u32[]{:S(2)}) collective-permute-start(bf16[272,128]{1,0:T(8,128)(2,1)S(1)} %get-tuple-element.55), channel_id=1, source_target_pairs={{2,0},{3,1},{0,2},{1,3},{6,4},{7,5},{4,6},{5,7},{10,8},{11,9},{8,1... | collective-permute-start | bytes 208904 | tf_op jit(solution)/shard_map/ppermute | solution.py:111
  69.5 9.8 %collective-permute-start.4 = (bf16[272,128]{1,0:T(8,128)(2,1)S(1)}, bf16[272,128]{1,0:T(8,128)(2,1)S(1)}, u32[]{:S(2)}, u32[]{:S(2)}) collective-permute-start(bf16[272,128]{1,0:T(8,128)(2,1)S(1)} %get-tuple-element.56), channel_id=1, source_target_pairs={{1,0},{2,1},{3,2},{0,3},{5,4},{6,5},{7,6},{4,7},{9,8},{10,9},{11,1... | collective-permute-start | bytes 208904 | tf_op jit(solution)/shard_map/ppermute | solution.py:111
  80.4 12.2 %all-to-all-start.3 = ((bf16[4,256,128]{2,1,0:T(8,128)(2,1)}), bf16[4,256,128]{2,1,0:T(8,128)(2,1)S(1)}, u32[]{:S(2)}, u32[]{:S(2)}) async-start(bf16[4,256,128]{2,1,0:T(8,128)(2,1)} %shard_map.115), calls=%async_computation.3 | async-start | bytes 524288 | tf_op jit(solution)/shard_map/all_to_all | solution.py:106
  95.1 11.4 %collective-permute-start.5 = (bf16[256,512]{1,0:T(8,128)(2,1)S(1)}, bf16[256,512]{1,0:T(8,128)(2,1)S(1)}, u32[]{:S(2)}, u32[]{:S(2)}) collective-permute-start(bf16[256,512]{1,0:T(8,128)(2,1)S(1)} %get-tuple-element.58.refs_0_), channel_id=1, source_target_pairs={{8,0},{12,4},{16,8},{20,12},{24,16},{28,20},{32,24},{36,28},{40,32... | collective-permute-start | bytes 786440 | tf_op jit(solution)/shard_map/ppermute | solution.py:111
  98.5 17.9 %all-to-all-start.4 = ((bf16[64,16,128]{2,1,0:T(8,128)(2,1)}), bf16[64,16,128]{2,1,0:T(8,128)(2,1)S(1)}, u32[]{:S(2)}, u32[]{:S(2)}) async-start(bf16[64,16,128]{2,1,0:T(8,128)(2,1)} %bitcast.7), calls=%async_computation.4 | async-start | bytes 524288 | tf_op jit(solution)/shard_map/all_to_all | solution.py:106
  109.9 0.8 copy-start.3
  110.7 12.1 %collective-permute-start.6 = (bf16[256,512]{1,0:T(8,128)(2,1)S(1)}, bf16[256,512]{1,0:T(8,128)(2,1)S(1)}, u32[]{:S(2)}, u32[]{:S(2)}) collective-permute-start(bf16[256,512]{1,0:T(8,128)(2,1)S(1)} %get-tuple-element.62), channel_id=1, source_target_pairs={{248,0},{252,4},{0,8},{4,12},{8,16},{12,20},{16,24},{20,28},{24,32... | collective-permute-start | bytes 786440 | tf_op jit(solution)/shard_map/ppermute | solution.py:111
  129.4 23.5 %all-to-all-start.5 = ((bf16[256,4,128]{2,1,0:T(4,128)(2,1)}), bf16[256,4,128]{2,1,0:T(4,128)(2,1)S(1)}, u32[]{:S(2)}, u32[]{:S(2)}) async-start(bf16[256,4,128]{2,1,0:T(4,128)(2,1)} %bitcast.9), calls=%async_computation.5 | async-start | bytes 524288 | tf_op jit(solution)/shard_map/all_to_all | solution.py:106
  136.3 11.9 %collective-permute-start.7 = (bf16[256,128]{1,0:T(8,128)(2,1)S(1)}, bf16[256,128]{1,0:T(8,128)(2,1)S(1)}, u32[]{:S(2)}, u32[]{:S(2)}) collective-permute-start(bf16[256,128]{1,0:T(8,128)(2,1)S(1)} %get-tuple-element.65), channel_id=1, source_target_pairs={{3,0},{0,1},{1,2},{2,3},{7,4},{4,5},{5,6},{6,7},{11,8},{8,9},{9,10... | collective-permute-start | bytes 196616 | tf_op jit(solution)/shard_map/ppermute | solution.py:111
  139.0 13.8 %collective-permute-start.8 = (bf16[256,128]{1,0:T(8,128)(2,1)S(1)}, bf16[256,128]{1,0:T(8,128)(2,1)S(1)}, u32[]{:S(2)}, u32[]{:S(2)}) collective-permute-start(bf16[256,128]{1,0:T(8,128)(2,1)S(1)} %get-tuple-element.66), channel_id=1, source_target_pairs={{2,0},{3,1},{0,2},{1,3},{6,4},{7,5},{4,6},{5,7},{10,8},{11,9},{8,1... | collective-permute-start | bytes 196616 | tf_op jit(solution)/shard_map/ppermute | solution.py:111
  143.4 9.5 %collective-permute-start.9 = (bf16[256,128]{1,0:T(8,128)(2,1)S(1)}, bf16[256,128]{1,0:T(8,128)(2,1)S(1)}, u32[]{:S(2)}, u32[]{:S(2)}) collective-permute-start(bf16[256,128]{1,0:T(8,128)(2,1)S(1)} %get-tuple-element.67), channel_id=1, source_target_pairs={{1,0},{2,1},{3,2},{0,3},{5,4},{6,5},{7,6},{4,7},{9,8},{10,9},{11,1... | collective-permute-start | bytes 196616 | tf_op jit(solution)/shard_map/ppermute | solution.py:111
  168.7 11.2 %collective-permute-start.10 = (bf16[256,512]{1,0:T(8,128)(2,1)S(1)}, bf16[256,512]{1,0:T(8,128)(2,1)S(1)}, u32[]{:S(2)}, u32[]{:S(2)}) collective-permute-start(bf16[256,512]{1,0:T(8,128)(2,1)S(1)} %get-tuple-element.71.refs_0_), channel_id=1, source_target_pairs={{12,0},{16,4},{20,8},{24,12},{28,16},{32,20},{36,24},{40,28},{44,3... | collective-permute-start | bytes 786440 | tf_op jit(solution)/shard_map/ppermute | solution.py:111
  175.7 13.7 %all-to-all-start.7 = ((bf16[64,16,128]{2,1,0:T(8,128)(2,1)}), bf16[64,16,128]{2,1,0:T(8,128)(2,1)S(1)}, u32[]{:S(2)}, u32[]{:S(2)}) async-start(bf16[64,16,128]{2,1,0:T(8,128)(2,1)} %bitcast.11), calls=%async_computation.7 | async-start | bytes 524288 | tf_op jit(solution)/shard_map/all_to_all | solution.py:106
  183.3 0.8 copy-start.2
  184.1 12.8 %collective-permute-start.11 = (bf16[256,512]{1,0:T(8,128)(2,1)S(1)}, bf16[256,512]{1,0:T(8,128)(2,1)S(1)}, u32[]{:S(2)}, u32[]{:S(2)}) collective-permute-start(bf16[256,512]{1,0:T(8,128)(2,1)S(1)} %get-tuple-element.75), channel_id=1, source_target_pairs={{244,0},{248,4},{252,8},{0,12},{4,16},{8,20},{12,24},{16,28},{20,3... | collective-permute-start | bytes 786440 | tf_op jit(solution)/shard_map/ppermute | solution.py:111
  207.5 2.2 collective-permute-start.18
  228.1 21.0 %all-to-all-start.8 = ((bf16[256,4,128]{2,1,0:T(4,128)(2,1)}), bf16[256,4,128]{2,1,0:T(4,128)(2,1)S(1)}, u32[]{:S(2)}, u32[]{:S(2)}) async-start(bf16[256,4,128]{2,1,0:T(4,128)(2,1)} %bitcast.13), calls=%async_computation.8 | async-start | bytes 524288 | tf_op jit(solution)/shard_map/all_to_all | solution.py:106
  249.1 38.0 %all-to-all-start.10 = ((bf16[64,16,512]{2,1,0:T(8,128)(2,1)}), bf16[64,16,512]{2,1,0:T(8,128)(2,1)S(1)}, u32[]{:S(2)}, u32[]{:S(2)}) async-start(bf16[64,16,512]{2,1,0:T(8,128)(2,1)} %shard_map.127), calls=%async_computation.10 | async-start | bytes 2097152 | tf_op jit(solution)/shard_map/all_to_all | solution.py:106
  254.3 15.3 %collective-permute-start.12 = (bf16[256,128]{1,0:T(8,128)(2,1)S(1)}, bf16[256,128]{1,0:T(8,128)(2,1)S(1)}, u32[]{:S(2)}, u32[]{:S(2)}) collective-permute-start(bf16[256,128]{1,0:T(8,128)(2,1)S(1)} %get-tuple-element.78), channel_id=1, source_target_pairs={{3,0},{0,1},{1,2},{2,3},{7,4},{4,5},{5,6},{6,7},{11,8},{8,9},{9,10... | collective-permute-start | bytes 196616 | tf_op jit(solution)/shard_map/ppermute | solution.py:111
  254.6 16.1 %collective-permute-start.13 = (bf16[256,128]{1,0:T(8,128)(2,1)S(1)}, bf16[256,128]{1,0:T(8,128)(2,1)S(1)}, u32[]{:S(2)}, u32[]{:S(2)}) collective-permute-start(bf16[256,128]{1,0:T(8,128)(2,1)S(1)} %get-tuple-element.79), channel_id=1, source_target_pairs={{2,0},{3,1},{0,2},{1,3},{6,4},{7,5},{4,6},{5,7},{10,8},{11,9},{8,1... | collective-permute-start | bytes 196616 | tf_op jit(solution)/shard_map/ppermute | solution.py:111
  257.0 13.7 %collective-permute-start.14 = (bf16[256,128]{1,0:T(8,128)(2,1)S(1)}, bf16[256,128]{1,0:T(8,128)(2,1)S(1)}, u32[]{:S(2)}, u32[]{:S(2)}) collective-permute-start(bf16[256,128]{1,0:T(8,128)(2,1)S(1)} %get-tuple-element.80), channel_id=1, source_target_pairs={{1,0},{2,1},{3,2},{0,3},{5,4},{6,5},{7,6},{4,7},{9,8},{10,9},{11,1... | collective-permute-start | bytes 196616 | tf_op jit(solution)/shard_map/ppermute | solution.py:111
  270.9 9.0 %collective-permute-start.17 = (bf16[256,128]{1,0:T(8,128)(2,1)S(1)}, bf16[256,128]{1,0:T(8,128)(2,1)S(1)}, u32[]{:S(2)}, u32[]{:S(2)}) collective-permute-start(bf16[256,128]{1,0:T(8,128)(2,1)S(1)} %bitcast.45), channel_id=1, source_target_pairs={{3,0},{0,1},{1,2},{2,3},{7,4},{4,5},{5,6},{6,7},{11,8},{8,9},{9,10... | collective-permute-start | bytes 196616 | tf_op jit(solution)/shard_map/ppermute | solution.py:111
  274.7 7.4 %collective-permute-start.16 = (bf16[256,128]{1,0:T(8,128)(2,1)S(1)}, bf16[256,128]{1,0:T(8,128)(2,1)S(1)}, u32[]{:S(2)}, u32[]{:S(2)}) collective-permute-start(bf16[256,128]{1,0:T(8,128)(2,1)S(1)} %bitcast.46), channel_id=1, source_target_pairs={{2,0},{3,1},{0,2},{1,3},{6,4},{7,5},{4,6},{5,7},{10,8},{11,9},{8,1... | collective-permute-start | bytes 196616 | tf_op jit(solution)/shard_map/ppermute | solution.py:111
  276.4 8.1 %collective-permute-start.15 = (bf16[256,128]{1,0:T(8,128)(2,1)S(1)}, bf16[256,128]{1,0:T(8,128)(2,1)S(1)}, u32[]{:S(2)}, u32[]{:S(2)}) collective-permute-start(bf16[256,128]{1,0:T(8,128)(2,1)S(1)} %bitcast.47), channel_id=1, source_target_pairs={{1,0},{2,1},{3,2},{0,3},{5,4},{6,5},{7,6},{4,7},{9,8},{10,9},{11,1... | collective-permute-start | bytes 196616 | tf_op jit(solution)/shard_map/ppermute | solution.py:111
  287.1 1.6 copy-start.7
  287.1 2.2 copy-start.8
where the time goes:
time: 294 us; the launch traced here: 292 us
  starting transfers between devices  105 us (36%)
  waiting for transfers between devices  79.6 us (27%)
  Pallas kernels  50.7 us (17%)
  blocking collectives  44.5 us (15%)
  local copies, waits for them, and re-layouts  6.34 us (2%)
  other arithmetic  4.65 us (2%)
    all_to_all x8, starting transfers between devices, all_ways(): return lax.all_to_all(block, axes, split_axis=0, concat_axis=0, tiled=True)  53.2 us
    ppermute x18, starting transfers between devices, from_behind(): lax.ppermute(block, axis, [((i - distance) % n, i) for i in range(n)])  52 us
    pallas_call x17, Pallas kernels, call(): pl.pallas_call(body, out_shape=shapes, in_specs=[hbm if i in late else ne...  50.7 us
    ppermute x18, waiting for transfers between devices, from_behind(): lax.ppermute(block, axis, [((i - distance) % n, i) for i in range(n)])  46.9 us
    all_to_all x3, blocking collectives, all_ways(): return lax.all_to_all(block, axes, split_axis=0, concat_axis=0, tiled=True)  44.5 us
    all_to_all x8, waiting for transfers between devices, all_ways(): return lax.all_to_all(block, axes, split_axis=0, concat_axis=0, tiled=True)  30.8 us
  transfers between devices with their start and end apart: 27, of which 17 were waited for; matrix products, arithmetic and copies ran while one was open for 1% of the time, Pallas kernels for 6%

commit v1 on v0

--- a/solution.py
+++ b/solution.py
@@ -171,19 +171,9 @@
         dtail_ref[cut, :] = nn(at, tq_ref[...]).astype(BF)
 
 
-def main_kernel(con_ref, tq_ref, n_ref, at_ref, par_ref, rel_ref, tail_ref, *refs):
-    neg_ref, an_ref, sum_ref, cut_ref = refs[-4:]
-    dneg_ref, g_ref = refs[0], refs[-5]
-    out_refs = refs[1:-5]
+def neg_kernel(con_ref, tq_ref, n_ref, neg_ref, an_ref, dneg_ref):
     slots, width = neg_ref.shape
     cuts = width // LANES
-    kinds = rel_ref.buffer.shape[0]
-    rows = par_ref.shape[0]
-    reps = cut_ref.shape[0]
-    idx_ref = None
-    if len(out_refs) > reps:
-        idx_ref, out_refs = out_refs[0], out_refs[1:]
-        dneg_ref, idx_ref = idx_ref, dneg_ref
     slot = iota((slots, con_ref.shape[0]), 0)
     row = iota((slots, con_ref.shape[0]), 1) - ((slot // NCAP) * (NCAP * cuts) + slot % NCAP)
 
@@ -194,39 +184,35 @@
         neg_ref[:, cut] = nn(perm, con_ref[...]).astype(BF)
 
     wide = dneg_ref.shape[1]
-    block = slots // 2
-
-    @pl.loop(0, 2)
-    def _(i):
-        cut = pl.ds(pl.multiple_of(i * block, block), block)
-        prob = jax.nn.sigmoid(nt(neg_ref[cut, :], tq_ref[...]))
-        an = (negative_weight * n_ref[:1] * prob).astype(BF)
-        an_ref[cut, :] = an
-        dneg = nn(an, tq_ref[...]).astype(BF)
-        for cs in range(width // wide):
-            start = pl.multiple_of(cs * slots + i * block, block)
-            dneg_ref[pl.ds(start, block), :] = dneg[:, cs * wide : (cs + 1) * wide]
-
-    rel = rel_ref.ready()
+    prob = jax.nn.sigmoid(nt(neg_ref[...], tq_ref[...]))
+    an_ref[...] = (negative_weight * n_ref[:1] * prob).astype(BF)
+    dneg = nn(an_ref[...], tq_ref[...]).astype(BF)
+    for cs in range(width // wide):
+        dneg_ref[cs * slots : (cs + 1) * slots, :] = dneg[:, cs * wide : (cs + 1) * wide]
+
+
+def head_kernel(at_ref, an_ref, par_ref, neg_ref, rel_ref, tail_ref, *refs):
+    sum_ref, cut_ref = refs[-2:]
+    g_ref = refs[-3]
+    reps, rows, wide = cut_ref.shape
+    out_refs = refs[-3 - reps : -3]
+    idx_refs = refs[: -3 - reps]
+    kinds = rel_ref.buffer.shape[0]
     sum_ref[...] = tail_ref[...].astype(F32)
-
-    half = rows // 2
-
-    @pl.loop(0, 2 * kinds)
-    def _(i):
-        cut = pl.ds(pl.multiple_of(i * half, half), half)
+    rel = None
+    for t in range(kinds):
+        cut = slice(t * rows, (t + 1) * rows)
         g = (tn(at_ref[:, cut], par_ref[...]) + tn(an_ref[:, cut], neg_ref[...])).astype(BF)
         g_ref.buffer[cut, :] = g
-        head = pl.ds(pl.multiple_of(i % 2 * half, half), half)
-        sum_ref[head, :] += nt(g, rel[i // 2])
-
+        rel = rel_ref.ready() if rel is None else rel
+        sum_ref[...] += nt(g, rel[t])
     g_ref.send()
     for cs in range(reps):
         cut_ref[cs] = sum_ref[:, cs * wide : (cs + 1) * wide].astype(BF)
     mine = lax.axis_index("rep")
     for s in range(reps):
         out_refs[s][:rows, :] = cut_ref[lax.rem(mine + s, reps)]
-        if idx_ref is not None:
+        for idx_ref in idx_refs:
             out_refs[s][rows:, :] = idx_ref[...]
 
 
@@ -357,27 +343,28 @@
         )
         dtail = from_behind(dtail, "dom", offset)
         lines = 0 if rnd else INDEX_LINES
-        dneg, *dhead, g = call(
-            main_kernel,
-            [((reps * slots, wide), BF)] + [((rows + lines, wide), BF)] * reps + [((kinds * rows, width), BF)],
+        neg, an, dneg = call(
+            neg_kernel,
+            [((slots, width), BF), ((slots, kinds * rows), BF), ((reps * slots, wide), BF)],
             con,
             tq,
             n,
+        )
+        dneg = all_ways(dneg.reshape(reps * parts, NCAP, wide), everyone).reshape(reps * slots, wide)
+        *dhead, g = call(
+            head_kernel,
+            [((rows + lines, wide), BF)] * reps + [((kinds * rows, width), BF)],
             at,
+            an,
             partner,
+            neg,
             rel_bf,
             dtail,
             *([] if rnd else [asked]),
-            late={5: kinds},
-            far=(1 + reps,),
-            scratch=[
-                pltpu.VMEM((slots, width), BF),
-                pltpu.VMEM((slots, kinds * rows), BF),
-                pltpu.VMEM((rows, width), F32),
-                pltpu.VMEM((reps, rows, wide), BF),
-            ],
+            late={4: kinds},
+            far=(reps,),
+            scratch=[pltpu.VMEM((rows, width), F32), pltpu.VMEM((reps, rows, wide), BF)],
         )
-        dneg = all_ways(dneg.reshape(reps * parts, NCAP, wide), everyone).reshape(reps * slots, wide)
         gs.append(g)
         for s in range(1, reps):
             dhead[s] = from_behind(dhead[s], "rep", s)

time: 294 us -> 304 us (1.034)
  starting transfers between devices: 105 us -> 123 us
  blocking collectives: 44.5 us -> 30.2 us
  waiting for transfers between devices: 79.6 us -> 92.8 us
  Pallas kernels: 50.7 us -> 46.3 us
    all_to_all x8 -> x9, starting transfers between devices: 53.2 us -> 76.9 us  [all_ways(): return lax.all_to_all(block, axes, split_axis=0, concat_axis=0, tiled=True)]
    all_to_all x3 -> x2, blocking collectives: 44.5 us -> 30.2 us  [all_ways(): return lax.all_to_all(block, axes, split_axis=0, concat_axis=0, tiled=True)]
    ppermute x18, waiting for transfers between devices: 46.9 us -> 58.7 us  [from_behind(): lax.ppermute(block, axis, [((i - distance) % n, i) for i in range(n)])]
    ppermute x18, starting transfers between devices: 52 us -> 45.9 us  [from_behind(): lax.ppermute(block, axis, [((i - distance) % n, i) for i in range(n)])]
    pallas_call x17 -> x20, Pallas kernels: 50.7 us -> 46.3 us  [call(): pl.pallas_call(body, out_shape=shapes, in_specs=[hbm if i in late else ne...]
    all_to_all x8 -> x9, waiting for transfers between devices: 30.8 us -> 32.2 us  [all_ways(): return lax.all_to_all(block, axes, split_axis=0, concat_axis=0, tiled=True)]
  transfers between devices with their start and end apart: 27 -> 28, of which waited for: 17 -> 19; matrix products, arithmetic and copies ran while one was open for 1% -> 1% of each run, Pallas kernels for 6% -> 8%
where the time goes in v1:
time: 304 us; the launch traced here: 302 us
  starting transfers between devices  123 us (40%)
  waiting for transfers between devices  92.8 us (31%)
  Pallas kernels  46.3 us (15%)
  blocking collectives  30.2 us (10%)
  other arithmetic  4.65 us (2%)
  local copies, waits for them, and re-layouts  4.61 us (2%)
    all_to_all x9, starting transfers between devices, all_ways(): return lax.all_to_all(block, axes, split_axis=0, concat_axis=0, tiled=True)  76.9 us
    ppermute x18, waiting for transfers between devices, from_behind(): lax.ppermute(block, axis, [((i - distance) % n, i) for i in range(n)])  58.7 us
    pallas_call x20, Pallas kernels, call(): pl.pallas_call(body, out_shape=shapes, in_specs=[hbm if i in late else ne...  46.3 us
    ppermute x18, starting transfers between devices, from_behind(): lax.ppermute(block, axis, [((i - distance) % n, i) for i in range(n)])  45.9 us
    all_to_all x9, waiting for transfers between devices, all_ways(): return lax.all_to_all(block, axes, split_axis=0, concat_axis=0, tiled=True)  32.2 us
    all_to_all x2, blocking collectives, all_ways(): return lax.all_to_all(block, axes, split_axis=0, concat_axis=0, tiled=True)  30.2 us
  transfers between devices with their start and end apart: 28, of which 19 were waited for; matrix products, arithmetic and copies ran while one was open for 1% of the time, Pallas kernels for 8%

profile of v1, /device:TPU:1, one launch (start us, length us, event | category | flops | bytes accessed | tf_op | source)
XLA Modules:
  0.0 302.4 jit_solution(1244017375903879540)
XLA Ops:
  2.3 10.3 %all-to-all-start = ((s32[64,1,12]{2,1,0:T(1,128)}), s32[64,1,12]{2,1,0:T(1,128)S(1)}, u32[]{:S(2)}, u32[]{:S(2)}) async-start(s32[64,1,12]{2,1,0:T(1,128)} %copy.21), calls=%async_computation | async-start | bytes 65536 | tf_op jit(solution)/shard_map/all_to_all | solution.py:106
  12.6 1.1 convert_element_type.10.refs_0_
  13.7 6.7 %all-to-all-done = s32[64,1,12]{2,1,0:T(1,128)S(1)} async-done(((s32[64,1,12]{2,1,0:T(1,128)}), s32[64,1,12]{2,1,0:T(1,128)S(1)}, u32[]{:S(2)}, u32[]{:S(2)}) %all-to-all-start) | async-done | bytes 3104 | tf_op jit(solution)/shard_map/all_to_all | solution.py:106
  20.7 2.2 shard_map.111
  22.9 4.7 %all-to-all-start.1 = ((bf16[64,16,128]{2,1,0:T(8,128)(2,1)}), bf16[64,16,128]{2,1,0:T(8,128)(2,1)S(1)}, u32[]{:S(2)}, u32[]{:S(2)}) async-start(bf16[64,16,128]{2,1,0:T(8,128)(2,1)} %bitcast.2), calls=%async_computation.1 | async-start | bytes 524288 | tf_op jit(solution)/shard_map/all_to_all | solution.py:106
  28.3 2.7 shard_map.112.refs_1_.refs_4_
  31.0 4.7 %collective-permute-done.refs_2_ = bf16[256,512]{1,0:T(8,128)(2,1)S(1)} collective-permute-done((bf16[256,512]{1,0:T(8,128)(2,1)S(1)}, bf16[256,512]{1,0:T(8,128)(2,1)S(1)}, u32[]{:S(2)}, u32[]{:S(2)}) %collective-permute-start) | collective-permute-done | bytes 262176 | tf_op jit(solution)/shard_map/ppermute | solution.py:111
  35.7 3.4 %shard_map.113 = (bf16[512,512]{1,0:T(8,128)(2,1)S(1)}, bf16[256,512]{1,0:T(8,128)(2,1)S(1)}, f32[8,512]{1,0:T(8,128)S(1)}, bf16[256,512]{1,0:T(8,128)(2,1)S(1)}) custom-call(bf16[256,512]{1,0:T(8,128)(2,1)S(1)} %convert_element_type.10.refs_0_, bf16[8,512,512]{2,1,0:T(8,128)(2,1)} %shard_map.112.refs_1_.refs_4_, ...), custom_call_target="tpu_custom_call" | custom-call | bytes 2665472 | tf_op jit(solution)/shard_map/pallas_call | solution.py:74
  39.1 2.5 shard_map.114
  41.6 15.2 %all-to-all-start.2 = ((bf16[256,4,128]{2,1,0:T(4,128)(2,1)}), bf16[256,4,128]{2,1,0:T(4,128)(2,1)S(1)}, u32[]{:S(2)}, u32[]{:S(2)}) async-start(bf16[256,4,128]{2,1,0:T(4,128)(2,1)} %bitcast.4), calls=%async_computation.2 | async-start | bytes 524288 | tf_op jit(solution)/shard_map/all_to_all | solution.py:106
  56.7 1.7 collective-permute-start.1
  58.7 4.6 %collective-permute-done.1.refs_5_ = bf16[256,512]{1,0:T(8,128)(2,1)S(1)} collective-permute-done((bf16[256,512]{1,0:T(8,128)(2,1)S(1)}, bf16[256,512]{1,0:T(8,128)(2,1)S(1)}, u32[]{:S(2)}, u32[]{:S(2)}) %collective-permute-start.1) | collective-permute-done | bytes 262176 | tf_op jit(solution)/shard_map/ppermute | solution.py:111
  63.3 2.6 shard_map.115
  65.9 2.1 collective-permute-start.2
  68.0 4.4 %collective-permute-start.3 = (bf16[272,128]{1,0:T(8,128)(2,1)S(1)}, bf16[272,128]{1,0:T(8,128)(2,1)S(1)}, u32[]{:S(2)}, u32[]{:S(2)}) collective-permute-start(bf16[272,128]{1,0:T(8,128)(2,1)S(1)} %get-tuple-element.63), channel_id=1, source_target_pairs={{2,0},{3,1},{0,2},{1,3},{6,4},{7,5},{4,6},{5,7},{10,8},{11,9},{8,1... | collective-permute-start | bytes 208904 | tf_op jit(solution)/shard_map/ppermute | solution.py:111
  72.4 2.5 collective-permute-start.4
  75.1 2.8 collective-permute-done.4.refs_4_.refs_8_
  78.9 4.3 %all-to-all-start.3 = ((bf16[4,256,128]{2,1,0:T(8,128)(2,1)}), bf16[4,256,128]{2,1,0:T(8,128)(2,1)S(1)}, u32[]{:S(2)}, u32[]{:S(2)}) async-start(bf16[4,256,128]{2,1,0:T(8,128)(2,1)} %shard_map.116), calls=%async_computation.3 | async-start | bytes 524288 | tf_op jit(solution)/shard_map/all_to_all | solution.py:106
  83.3 8.3 %all-to-all-done.3.refs_0_ = bf16[4,256,128]{2,1,0:T(8,128)(2,1)S(1)} async-done(((bf16[4,256,128]{2,1,0:T(8,128)(2,1)}), bf16[4,256,128]{2,1,0:T(8,128)(2,1)S(1)}, u32[]{:S(2)}, u32[]{:S(2)}) %all-to-all-start.3) | async-done | bytes 262176 | tf_op jit(solution)/shard_map/all_to_all | solution.py:106
  91.6 2.5 shard_map.117
  94.1 15.9 %all-to-all-start.4 = ((bf16[64,16,128]{2,1,0:T(8,128)(2,1)}), bf16[64,16,128]{2,1,0:T(8,128)(2,1)S(1)}, u32[]{:S(2)}, u32[]{:S(2)}) async-start(bf16[64,16,128]{2,1,0:T(8,128)(2,1)} %bitcast.7), calls=%async_computation.4 | async-start | bytes 524288 | tf_op jit(solution)/shard_map/all_to_all | solution.py:106
  110.0 6.1 %collective-permute-start.5 = (bf16[256,512]{1,0:T(8,128)(2,1)S(1)}, bf16[256,512]{1,0:T(8,128)(2,1)S(1)}, u32[]{:S(2)}, u32[]{:S(2)}) collective-permute-start(bf16[256,512]{1,0:T(8,128)(2,1)S(1)} %get-tuple-element.66.refs_0_), channel_id=1, source_target_pairs={{8,0},{12,4},{16,8},{20,12},{24,16},{28,20},{32,24},{36,28},{40,32... | collective-permute-start | bytes 786440 | tf_op jit(solution)/shard_map/ppermute | solution.py:111
  116.1 5.3 %collective-permute-done.5.refs_2_ = bf16[256,512]{1,0:T(8,128)(2,1)S(1)} collective-permute-done((bf16[256,512]{1,0:T(8,128)(2,1)S(1)}, bf16[256,512]{1,0:T(8,128)(2,1)S(1)}, u32[]{:S(2)}, u32[]{:S(2)}) %collective-permute-start.5) | collective-permute-done | bytes 262176 | tf_op jit(solution)/shard_map/ppermute | solution.py:111
  121.4 3.4 %shard_map.118 = (bf16[512,512]{1,0:T(8,128)(2,1)S(1)}, bf16[256,512]{1,0:T(8,128)(2,1)S(1)}, f32[8,512]{1,0:T(8,128)S(1)}, bf16[256,512]{1,0:T(8,128)(2,1)S(1)}) custom-call(bf16[256,512]{1,0:T(8,128)(2,1)S(1)} %get-tuple-element.66.refs_0_, bf16[8,512,512]{2,1,0:T(8,128)(2,1)} %shard_map.112.refs_1_.refs_4_, ...), custom_call_target="tpu_custom_call" | custom-call | bytes 2665472 | tf_op jit(solution)/shard_map/pallas_call | solution.py:74
  124.8 2.5 shard_map.119
  127.3 9.8 %all-to-all-start.5 = ((bf16[256,4,128]{2,1,0:T(4,128)(2,1)}), bf16[256,4,128]{2,1,0:T(4,128)(2,1)S(1)}, u32[]{:S(2)}, u32[]{:S(2)}) async-start(bf16[256,4,128]{2,1,0:T(4,128)(2,1)} %bitcast.9), calls=%async_computation.5 | async-start | bytes 524288 | tf_op jit(solution)/shard_map/all_to_all | solution.py:106
  137.1 1.4 collective-permute-start.6
  138.5 15.6 %collective-permute-done.6.refs_5_ = bf16[256,512]{1,0:T(8,128)(2,1)S(1)} collective-permute-done((bf16[256,512]{1,0:T(8,128)(2,1)S(1)}, bf16[256,512]{1,0:T(8,128)(2,1)S(1)}, u32[]{:S(2)}, u32[]{:S(2)}) %collective-permute-start.6) | collective-permute-done | bytes 262176 | tf_op jit(solution)/shard_map/ppermute | solution.py:111
  154.2 2.6 shard_map.120
  156.7 2.0 collective-permute-start.7
  158.8 2.9 collective-permute-start.8
  161.6 3.3 %collective-permute-start.9 = (bf16[256,128]{1,0:T(8,128)(2,1)S(1)}, bf16[256,128]{1,0:T(8,128)(2,1)S(1)}, u32[]{:S(2)}, u32[]{:S(2)}) collective-permute-start(bf16[256,128]{1,0:T(8,128)(2,1)S(1)} %get-tuple-element.77), channel_id=1, source_target_pairs={{1,0},{2,1},{3,2},{0,3},{5,4},{6,5},{7,6},{4,7},{9,8},{10,9},{11,1... | collective-permute-start | bytes 196616 | tf_op jit(solution)/shard_map/ppermute | solution.py:111
  165.0 1.1 collective-permute-done.8.refs_3_
  166.1 1.8 collective-permute-done.9.refs_4_
  168.2 13.7 %all_to_all.59.refs_0_ = bf16[4,256,128]{2,1,0:T(8,128)(2,1)S(1)} all-to-all(bf16[4,256,128]{2,1,0:T(8,128)(2,1)S(1)} %shard_map.121), channel_id=1, replica_groups=mesh['dom'=64,'rep'=4] {'rep'}, dimensions={0} | all-to-all | bytes 524288 | tf_op jit(solution)/shard_map/all_to_all | solution.py:106
  182.0 3.4 %shard_map.122 = (f32[256,1]{1,0:T(8,128)S(1)}, bf16[256,512]{1,0:T(8,128)(2,1)S(1)}, bf16[1024,128]{1,0:T(8,128)(2,1)}, f32[2048,512]{1,0:T(8,128)}, bf16[4096,512]{1,0:T(8,128)(2,1)}) custom-call(bf16[4,256,128]{2,1,0:T(8,128)(2,1)S(1)} %all_to_all.59.refs_0_, f32[2048,512]{1,0:T(8,128)} %get-tuple-element.78.refs_1_, ...), custom_call_target="tpu_custom_call" | custom-call | bytes 2102272 | tf_op jit(solution)/shard_map/pallas_call | solution.py:74
  185.4 3.1 %collective-permute-start.10 = (bf16[256,512]{1,0:T(8,128)(2,1)S(1)}, bf16[256,512]{1,0:T(8,128)(2,1)S(1)}, u32[]{:S(2)}, u32[]{:S(2)}) collective-permute-start(bf16[256,512]{1,0:T(8,128)(2,1)S(1)} %get-tuple-element.81.refs_0_), channel_id=1, source_target_pairs={{12,0},{16,4},{20,8},{24,12},{28,16},{32,20},{36,24},{40,28},{44,3... | collective-permute-start | bytes 786440 | tf_op jit(solution)/shard_map/ppermute | solution.py:111
  188.5 5.5 %all-to-all-start.7 = ((bf16[64,16,128]{2,1,0:T(8,128)(2,1)}), bf16[64,16,128]{2,1,0:T(8,128)(2,1)S(1)}, u32[]{:S(2)}, u32[]{:S(2)}) async-start(bf16[64,16,128]{2,1,0:T(8,128)(2,1)} %bitcast.11), calls=%async_computation.7 | async-start | bytes 524288 | tf_op jit(solution)/shard_map/all_to_all | solution.py:106
  194.6 3.4 %shard_map.123 = (bf16[512,512]{1,0:T(8,128)(2,1)S(1)}, bf16[256,512]{1,0:T(8,128)(2,1)S(1)}, f32[8,512]{1,0:T(8,128)S(1)}, bf16[256,512]{1,0:T(8,128)(2,1)S(1)}) custom-call(bf16[256,512]{1,0:T(8,128)(2,1)S(1)} %get-tuple-element.81.refs_0_, bf16[8,512,512]{2,1,0:T(8,128)(2,1)} %shard_map.112.refs_1_.refs_4_, ...), custom_call_target="tpu_custom_call" | custom-call | bytes 2665472 | tf_op jit(solution)/shard_map/pallas_call | solution.py:74
  198.0 2.9 collective-permute-start.11
  200.9 2.9 all-to-all-done.7
  203.8 2.5 shard_map.124
  206.3 5.0 %collective-permute-done.11.refs_5_ = bf16[256,512]{1,0:T(8,128)(2,1)S(1)} collective-permute-done((bf16[256,512]{1,0:T(8,128)(2,1)S(1)}, bf16[256,512]{1,0:T(8,128)(2,1)S(1)}, u32[]{:S(2)}, u32[]{:S(2)}) %collective-permute-start.11) | collective-permute-done | bytes 262176 | tf_op jit(solution)/shard_map/ppermute | solution.py:111
  211.4 2.6 shard_map.125
  213.9 4.0 %shard_map.128 = (bf16[512,512]{1,0:T(8,128)(2,1)S(1)}, f32[2048,512]{1,0:T(8,128)}) custom-call(f32[256,512]{1,0:T(8,128)S(1)} %copy-done, bf16[4096,512]{1,0:T(8,128)(2,1)} %get-tuple-element.97.refs_1_, bf16[4096,512]{1,0:T(8,128)(2,1)} %get-tuple-element.98.refs_2_, bf16[4096,512]{1,0:T(8,128)(2,1)} %get-tuple-element.99.refs_3_, ...), custom_call_target="tpu_custom_call" | custom-call | bytes 4194304 | tf_op jit(solution)/shard_map/pallas_call | solution.py:74
  218.0 1.9 collective-permute-done.18.refs_1_
  219.9 1.4 shard_map.129
  221.3 16.5 %all_to_all.60.refs_0_ = bf16[64,8,512]{2,1,0:T(8,128)(2,1)S(1)} all-to-all(bf16[64,8,512]{2,1,0:T(8,128)(2,1)S(1)} %bitcast.38), channel_id=1, replica_groups=mesh['dom'=64,'rep'=4] {'dom'}, dimensions={0} | all-to-all | bytes 1048576 | tf_op jit(solution)/shard_map/all_to_all | solution.py:106
  237.8 6.0 %all-to-all-start.8 = ((bf16[256,4,128]{2,1,0:T(4,128)(2,1)}), bf16[256,4,128]{2,1,0:T(4,128)(2,1)S(1)}, u32[]{:S(2)}, u32[]{:S(2)}) async-start(bf16[256,4,128]{2,1,0:T(4,128)(2,1)} %bitcast.13), calls=%async_computation.8 | async-start | bytes 524288 | tf_op jit(solution)/shard_map/all_to_all | solution.py:106
  243.8 1.1 shard_map.130
  244.9 14.3 %all-to-all-done.8 = bf16[256,4,128]{2,1,0:T(4,128)(2,1)S(1)} async-done(((bf16[256,4,128]{2,1,0:T(4,128)(2,1)}), bf16[256,4,128]{2,1,0:T(4,128)(2,1)S(1)}, u32[]{:S(2)}, u32[]{:S(2)}) %all-to-all-start.8) | async-done | bytes 262176 | tf_op jit(solution)/shard_map/all_to_all | solution.py:106
  259.2 5.2 %all-to-all-start.10 = ((bf16[64,16,512]{2,1,0:T(8,128)(2,1)}), bf16[64,16,512]{2,1,0:T(8,128)(2,1)S(1)}, u32[]{:S(2)}, u32[]{:S(2)}) async-start(bf16[64,16,512]{2,1,0:T(8,128)(2,1)} %shard_map.130), calls=%async_computation.10 | async-start | bytes 2097152 | tf_op jit(solution)/shard_map/all_to_all | solution.py:106
  264.7 2.4 collective-permute-start.13
  267.1 1.3 collective-permute-start.14
  268.4 11.3 %collective-permute-done.12.refs_2_ = bf16[256,128]{1,0:T(8,128)(2,1)S(1)} collective-permute-done((bf16[256,128]{1,0:T(8,128)(2,1)S(1)}, bf16[256,128]{1,0:T(8,128)(2,1)S(1)}, u32[]{:S(2)}, u32[]{:S(2)}) %collective-permute-start.12) | collective-permute-done | bytes 65568 | tf_op jit(solution)/shard_map/ppermute | solution.py:111
  279.7 1.0 collective-permute-done.13.refs_3_
  281.1 3.7 %collective-permute-start.17 = (bf16[256,128]{1,0:T(8,128)(2,1)S(1)}, bf16[256,128]{1,0:T(8,128)(2,1)S(1)}, u32[]{:S(2)}, u32[]{:S(2)}) collective-permute-start(bf16[256,128]{1,0:T(8,128)(2,1)S(1)} %bitcast.45), channel_id=1, source_target_pairs={{3,0},{0,1},{1,2},{2,3},{7,4},{4,5},{5,6},{6,7},{11,8},{8,9},{9,10... | collective-permute-start | bytes 196616 | tf_op jit(solution)/shard_map/ppermute | solution.py:111
  284.9 1.7 collective-permute-start.16
  286.6 3.5 %collective-permute-start.15 = (bf16[256,128]{1,0:T(8,128)(2,1)S(1)}, bf16[256,128]{1,0:T(8,128)(2,1)S(1)}, u32[]{:S(2)}, u32[]{:S(2)}) collective-permute-start(bf16[256,128]{1,0:T(8,128)(2,1)S(1)} %bitcast.47), channel_id=1, source_target_pairs={{1,0},{2,1},{3,2},{0,3},{5,4},{6,5},{7,6},{4,7},{9,8},{10,9},{11,1... | collective-permute-start | bytes 196616 | tf_op jit(solution)/shard_map/ppermute | solution.py:111
  290.1 2.2 collective-permute-done.16.refs_2_
  292.2 2.4 collective-permute-done.15.refs_1_
  294.7 2.0 shard_map.127
  297.8 1.0 copy-done.4
  299.4 3.0 fusion.2
  (49 shorter events, 7.5 us)
Async XLA Ops:
  2.3 18.1 %all-to-all-start = ((s32[64,1,12]{2,1,0:T(1,128)}), s32[64,1,12]{2,1,0:T(1,128)S(1)}, u32[]{:S(2)}, u32[]{:S(2)}) async-start(s32[64,1,12]{2,1,0:T(1,128)} %copy.21), calls=%async_computation | async-start | bytes 65536 | tf_op jit(solution)/shard_map/all_to_all | solution.py:106
  22.9 16.2 %all-to-all-start.1 = ((bf16[64,16,128]{2,1,0:T(8,128)(2,1)}), bf16[64,16,128]{2,1,0:T(8,128)(2,1)S(1)}, u32[]{:S(2)}, u32[]{:S(2)}) async-start(bf16[64,16,128]{2,1,0:T(8,128)(2,1)} %bitcast.2), calls=%async_computation.1 | async-start | bytes 524288 | tf_op jit(solution)/shard_map/all_to_all | solution.py:106
  27.6 8.1 %copy-start.1 = (s32[3,768]{1,0:T(4,128)S(1)}, s32[3,768]{1,0:T(4,128)}, u32[]{:S(2)}) copy-start(s32[3,768]{1,0:T(4,128)} %refs_3_.5) | copy-start | bytes 27652
  27.6 8.1 %copy-start.2 = (s32[3,768]{1,0:T(4,128)S(1)}, s32[3,768]{1,0:T(4,128)}, u32[]{:S(2)}) copy-start(s32[3,768]{1,0:T(4,128)} %refs_4_.5) | copy-start | bytes 27652
  27.6 8.1 %copy-start.3 = (s32[3,768]{1,0:T(4,128)S(1)}, s32[3,768]{1,0:T(4,128)}, u32[]{:S(2)}) copy-start(s32[3,768]{1,0:T(4,128)} %refs_5_.5) | copy-start | bytes 27652
  27.6 8.0 %collective-permute-start = (bf16[256,512]{1,0:T(8,128)(2,1)S(1)}, bf16[256,512]{1,0:T(8,128)(2,1)S(1)}, u32[]{:S(2)}, u32[]{:S(2)}) collective-permute-start(bf16[256,512]{1,0:T(8,128)(2,1)S(1)} %convert_element_type.10.refs_0_), channel_id=1, source_target_pairs={{4,0},{8,4},{12,8},{16,12},{20,16},{24,20},{28,24},{32,28},{36,32}... | collective-permute-start | bytes 786440 | tf_op jit(solution)/shard_map/ppermute | solution.py:111
  41.6 36.3 %all-to-all-start.2 = ((bf16[256,4,128]{2,1,0:T(4,128)(2,1)}), bf16[256,4,128]{2,1,0:T(4,128)(2,1)S(1)}, u32[]{:S(2)}, u32[]{:S(2)}) async-start(bf16[256,4,128]{2,1,0:T(4,128)(2,1)} %bitcast.4), calls=%async_computation.2 | async-start | bytes 524288 | tf_op jit(solution)/shard_map/all_to_all | solution.py:106
  56.7 6.6 %collective-permute-start.1 = (bf16[256,512]{1,0:T(8,128)(2,1)S(1)}, bf16[256,512]{1,0:T(8,128)(2,1)S(1)}, u32[]{:S(2)}, u32[]{:S(2)}) collective-permute-start(bf16[256,512]{1,0:T(8,128)(2,1)S(1)} %get-tuple-element.60), channel_id=1, source_target_pairs={{252,0},{0,4},{4,8},{8,12},{12,16},{16,20},{20,24},{24,28},{28,32}... | collective-permute-start | bytes 786440 | tf_op jit(solution)/shard_map/ppermute | solution.py:111
  63.3 19.8 %copy-start.6 = (f32[256]{0:T(256)S(1)}, f32[256]{0:T(256)}, u32[]{:S(2)}) copy-start(f32[256]{0:T(256)} %param.9) | copy-start | bytes 3076
  65.9 25.6 %copy-start = (f32[256,512]{1,0:T(8,128)S(1)}, f32[256,512]{1,0:T(8,128)}, u32[]{:S(2)}) copy-start(f32[256,512]{1,0:T(8,128)} %refs_0_.3) | copy-start | bytes 1572868
  65.9 8.9 %collective-permute-start.2 = (bf16[272,128]{1,0:T(8,128)(2,1)S(1)}, bf16[272,128]{1,0:T(8,128)(2,1)S(1)}, u32[]{:S(2)}, u32[]{:S(2)}) collective-permute-start(bf16[272,128]{1,0:T(8,128)(2,1)S(1)} %get-tuple-element.62), channel_id=1, source_target_pairs={{3,0},{0,1},{1,2},{2,3},{7,4},{4,5},{5,6},{6,7},{11,8},{8,9},{9,10... | collective-permute-start | bytes 208904 | tf_op jit(solution)/shard_map/ppermute | solution.py:111
  68.0 7.1 %collective-permute-start.3 = (bf16[272,128]{1,0:T(8,128)(2,1)S(1)}, bf16[272,128]{1,0:T(8,128)(2,1)S(1)}, u32[]{:S(2)}, u32[]{:S(2)}) collective-permute-start(bf16[272,128]{1,0:T(8,128)(2,1)S(1)} %get-tuple-element.63), channel_id=1, source_target_pairs={{2,0},{3,1},{0,2},{1,3},{6,4},{7,5},{4,6},{5,7},{10,8},{11,9},{8,1... | collective-permute-start | bytes 208904 | tf_op jit(solution)/shard_map/ppermute | solution.py:111
  72.4 5.5 %collective-permute-start.4 = (bf16[272,128]{1,0:T(8,128)(2,1)S(1)}, bf16[272,128]{1,0:T(8,128)(2,1)S(1)}, u32[]{:S(2)}, u32[]{:S(2)}) collective-permute-start(bf16[272,128]{1,0:T(8,128)(2,1)S(1)} %get-tuple-element.64), channel_id=1, source_target_pairs={{1,0},{2,1},{3,2},{0,3},{5,4},{6,5},{7,6},{4,7},{9,8},{10,9},{11,1... | collective-permute-start | bytes 208904 | tf_op jit(solution)/shard_map/ppermute | solution.py:111
  78.9 12.7 %all-to-all-start.3 = ((bf16[4,256,128]{2,1,0:T(8,128)(2,1)}), bf16[4,256,128]{2,1,0:T(8,128)(2,1)S(1)}, u32[]{:S(2)}, u32[]{:S(2)}) async-start(bf16[4,256,128]{2,1,0:T(8,128)(2,1)} %shard_map.116), calls=%async_computation.3 | async-start | bytes 524288 | tf_op jit(solution)/shard_map/all_to_all | solution.py:106
  94.1 30.7 %all-to-all-start.4 = ((bf16[64,16,128]{2,1,0:T(8,128)(2,1)}), bf16[64,16,128]{2,1,0:T(8,128)(2,1)S(1)}, u32[]{:S(2)}, u32[]{:S(2)}) async-start(bf16[64,16,128]{2,1,0:T(8,128)(2,1)} %bitcast.7), calls=%async_computation.4 | async-start | bytes 524288 | tf_op jit(solution)/shard_map/all_to_all | solution.py:106
  110.0 11.3 %collective-permute-start.5 = (bf16[256,512]{1,0:T(8,128)(2,1)S(1)}, bf16[256,512]{1,0:T(8,128)(2,1)S(1)}, u32[]{:S(2)}, u32[]{:S(2)}) collective-permute-start(bf16[256,512]{1,0:T(8,128)(2,1)S(1)} %get-tuple-element.66.refs_0_), channel_id=1, source_target_pairs={{8,0},{12,4},{16,8},{20,12},{24,16},{28,20},{32,24},{36,28},{40,32... | collective-permute-start | bytes 786440 | tf_op jit(solution)/shard_map/ppermute | solution.py:111
  127.3 40.6 %all-to-all-start.5 = ((bf16[256,4,128]{2,1,0:T(4,128)(2,1)}), bf16[256,4,128]{2,1,0:T(4,128)(2,1)S(1)}, u32[]{:S(2)}, u32[]{:S(2)}) async-start(bf16[256,4,128]{2,1,0:T(4,128)(2,1)} %bitcast.9), calls=%async_computation.5 | async-start | bytes 524288 | tf_op jit(solution)/shard_map/all_to_all | solution.py:106
  137.1 17.1 %collective-permute-start.6 = (bf16[256,512]{1,0:T(8,128)(2,1)S(1)}, bf16[256,512]{1,0:T(8,128)(2,1)S(1)}, u32[]{:S(2)}, u32[]{:S(2)}) collective-permute-start(bf16[256,512]{1,0:T(8,128)(2,1)S(1)} %get-tuple-element.73), channel_id=1, source_target_pairs={{248,0},{252,4},{0,8},{4,12},{8,16},{12,20},{16,24},{20,28},{24,32... | collective-permute-start | bytes 786440 | tf_op jit(solution)/shard_map/ppermute | solution.py:111
  156.7 8.2 %collective-permute-start.7 = (bf16[256,128]{1,0:T(8,128)(2,1)S(1)}, bf16[256,128]{1,0:T(8,128)(2,1)S(1)}, u32[]{:S(2)}, u32[]{:S(2)}) collective-permute-start(bf16[256,128]{1,0:T(8,128)(2,1)S(1)} %get-tuple-element.75), channel_id=1, source_target_pairs={{3,0},{0,1},{1,2},{2,3},{7,4},{4,5},{5,6},{6,7},{11,8},{8,9},{9,10... | collective-permute-start | bytes 196616 | tf_op jit(solution)/shard_map/ppermute | solution.py:111
  158.8 7.4 %collective-permute-start.8 = (bf16[256,128]{1,0:T(8,128)(2,1)S(1)}, bf16[256,128]{1,0:T(8,128)(2,1)S(1)}, u32[]{:S(2)}, u32[]{:S(2)}) collective-permute-start(bf16[256,128]{1,0:T(8,128)(2,1)S(1)} %get-tuple-element.76), channel_id=1, source_target_pairs={{2,0},{3,1},{0,2},{1,3},{6,4},{7,5},{4,6},{5,7},{10,8},{11,9},{8,1... | collective-permute-start | bytes 196616 | tf_op jit(solution)/shard_map/ppermute | solution.py:111
  161.6 6.3 %collective-permute-start.9 = (bf16[256,128]{1,0:T(8,128)(2,1)S(1)}, bf16[256,128]{1,0:T(8,128)(2,1)S(1)}, u32[]{:S(2)}, u32[]{:S(2)}) collective-permute-start(bf16[256,128]{1,0:T(8,128)(2,1)S(1)} %get-tuple-element.77), channel_id=1, source_target_pairs={{1,0},{2,1},{3,2},{0,3},{5,4},{6,5},{7,6},{4,7},{9,8},{10,9},{11,1... | collective-permute-start | bytes 196616 | tf_op jit(solution)/shard_map/ppermute | solution.py:111
  185.4 9.3 %collective-permute-start.10 = (bf16[256,512]{1,0:T(8,128)(2,1)S(1)}, bf16[256,512]{1,0:T(8,128)(2,1)S(1)}, u32[]{:S(2)}, u32[]{:S(2)}) collective-permute-start(bf16[256,512]{1,0:T(8,128)(2,1)S(1)} %get-tuple-element.81.refs_0_), channel_id=1, source_target_pairs={{12,0},{16,4},{20,8},{24,12},{28,16},{32,20},{36,24},{40,28},{44,3... | collective-permute-start | bytes 786440 | tf_op jit(solution)/shard_map/ppermute | solution.py:111
  188.5 15.3 %all-to-all-start.7 = ((bf16[64,16,128]{2,1,0:T(8,128)(2,1)}), bf16[64,16,128]{2,1,0:T(8,128)(2,1)S(1)}, u32[]{:S(2)}, u32[]{:S(2)}) async-start(bf16[64,16,128]{2,1,0:T(8,128)(2,1)} %bitcast.11), calls=%async_computation.7 | async-start | bytes 524288 | tf_op jit(solution)/shard_map/all_to_all | solution.py:106
  198.0 13.3 %collective-permute-start.11 = (bf16[256,512]{1,0:T(8,128)(2,1)S(1)}, bf16[256,512]{1,0:T(8,128)(2,1)S(1)}, u32[]{:S(2)}, u32[]{:S(2)}) collective-permute-start(bf16[256,512]{1,0:T(8,128)(2,1)S(1)} %get-tuple-element.88), channel_id=1, source_target_pairs={{244,0},{248,4},{252,8},{0,12},{4,16},{8,20},{12,24},{16,28},{20,3... | collective-permute-start | bytes 786440 | tf_op jit(solution)/shard_map/ppermute | solution.py:111
  217.9 2.0 collective-permute-start.18
  237.8 21.4 %all-to-all-start.8 = ((bf16[256,4,128]{2,1,0:T(4,128)(2,1)}), bf16[256,4,128]{2,1,0:T(4,128)(2,1)S(1)}, u32[]{:S(2)}, u32[]{:S(2)}) async-start(bf16[256,4,128]{2,1,0:T(4,128)(2,1)} %bitcast.13), calls=%async_computation.8 | async-start | bytes 524288 | tf_op jit(solution)/shard_map/all_to_all | solution.py:106
  259.2 38.0 %all-to-all-start.10 = ((bf16[64,16,512]{2,1,0:T(8,128)(2,1)}), bf16[64,16,512]{2,1,0:T(8,128)(2,1)S(1)}, u32[]{:S(2)}, u32[]{:S(2)}) async-start(bf16[64,16,512]{2,1,0:T(8,128)(2,1)} %shard_map.130), calls=%async_computation.10 | async-start | bytes 2097152 | tf_op jit(solution)/shard_map/all_to_all | solution.py:106
  264.5 15.3 %collective-permute-start.12 = (bf16[256,128]{1,0:T(8,128)(2,1)S(1)}, bf16[256,128]{1,0:T(8,128)(2,1)S(1)}, u32[]{:S(2)}, u32[]{:S(2)}) collective-permute-start(bf16[256,128]{1,0:T(8,128)(2,1)S(1)} %get-tuple-element.90), channel_id=1, source_target_pairs={{3,0},{0,1},{1,2},{2,3},{7,4},{4,5},{5,6},{6,7},{11,8},{8,9},{9,10... | collective-permute-start | bytes 196616 | tf_op jit(solution)/shard_map/ppermute | solution.py:111
  264.7 16.1 %collective-permute-start.13 = (bf16[256,128]{1,0:T(8,128)(2,1)S(1)}, bf16[256,128]{1,0:T(8,128)(2,1)S(1)}, u32[]{:S(2)}, u32[]{:S(2)}) collective-permute-start(bf16[256,128]{1,0:T(8,128)(2,1)S(1)} %get-tuple-element.91), channel_id=1, source_target_pairs={{2,0},{3,1},{0,2},{1,3},{6,4},{7,5},{4,6},{5,7},{10,8},{11,9},{8,1... | collective-permute-start | bytes 196616 | tf_op jit(solution)/shard_map/ppermute | solution.py:111
  267.1 13.7 %collective-permute-start.14 = (bf16[256,128]{1,0:T(8,128)(2,1)S(1)}, bf16[256,128]{1,0:T(8,128)(2,1)S(1)}, u32[]{:S(2)}, u32[]{:S(2)}) collective-permute-start(bf16[256,128]{1,0:T(8,128)(2,1)S(1)} %get-tuple-element.92), channel_id=1, source_target_pairs={{1,0},{2,1},{3,2},{0,3},{5,4},{6,5},{7,6},{4,7},{9,8},{10,9},{11,1... | collective-permute-start | bytes 196616 | tf_op jit(solution)/shard_map/ppermute | solution.py:111
  281.1 8.9 %collective-permute-start.17 = (bf16[256,128]{1,0:T(8,128)(2,1)S(1)}, bf16[256,128]{1,0:T(8,128)(2,1)S(1)}, u32[]{:S(2)}, u32[]{:S(2)}) collective-permute-start(bf16[256,128]{1,0:T(8,128)(2,1)S(1)} %bitcast.45), channel_id=1, source_target_pairs={{3,0},{0,1},{1,2},{2,3},{7,4},{4,5},{5,6},{6,7},{11,8},{8,9},{9,10... | collective-permute-start | bytes 196616 | tf_op jit(solution)/shard_map/ppermute | solution.py:111
  284.9 7.4 %collective-permute-start.16 = (bf16[256,128]{1,0:T(8,128)(2,1)S(1)}, bf16[256,128]{1,0:T(8,128)(2,1)S(1)}, u32[]{:S(2)}, u32[]{:S(2)}) collective-permute-start(bf16[256,128]{1,0:T(8,128)(2,1)S(1)} %bitcast.46), channel_id=1, source_target_pairs={{2,0},{3,1},{0,2},{1,3},{6,4},{7,5},{4,6},{5,7},{10,8},{11,9},{8,1... | collective-permute-start | bytes 196616 | tf_op jit(solution)/shard_map/ppermute | solution.py:111
  286.6 8.1 %collective-permute-start.15 = (bf16[256,128]{1,0:T(8,128)(2,1)S(1)}, bf16[256,128]{1,0:T(8,128)(2,1)S(1)}, u32[]{:S(2)}, u32[]{:S(2)}) collective-permute-start(bf16[256,128]{1,0:T(8,128)(2,1)S(1)} %bitcast.47), channel_id=1, source_target_pairs={{1,0},{2,1},{3,2},{0,3},{5,4},{6,5},{7,6},{4,7},{9,8},{10,9},{11,1... | collective-permute-start | bytes 196616 | tf_op jit(solution)/shard_map/ppermute | solution.py:111
  297.2 1.6 copy-start.4
  297.2 2.2 copy-start.5

commit v2 on v1

--- a/solution.py
+++ b/solution.py
@@ -111,24 +111,20 @@
     return lax.ppermute(block, axis, [((i - distance) % n, i) for i in range(n)])
 
 
-def fill_container(out_ref, sel_ref, ent_ref, idx_ref, rnd):
-    rows, width = ent_ref.shape
-    cuts = width // LANES
-    sel_ref[...] = tn(one_hot_rows(rows, idx_ref[rnd : rnd + 1]), ent_ref[...]).astype(BF)
-    slots = sel_ref.shape[0]
-    block = out_ref.shape[0] // cuts
-    line = iota((block, slots), 0)
-    which = (line // NCAP) % cuts
-    slot = line // (NCAP * cuts) * NCAP + line % NCAP - iota((block, slots), 1)
-
-    @pl.loop(0, cuts)
-    def _(i):
-        first = i * (block // cuts)
-        out = jnp.zeros((block, LANES), F32)
-        for cs in range(cuts):
-            perm = ((slot + first == 0) & (which == cs)).astype(F32).astype(BF)
-            out = out + nn(perm, sel_ref[:, cs * LANES : (cs + 1) * LANES])
-        out_ref[pl.ds(pl.multiple_of(i * block, block), block), :] = out.astype(BF)
+def container_cells(parts, cuts):
+    for cs in range(cuts):
+        for k in range(NCAP):
+            yield cs, pl.ds(k, parts, stride=NCAP), pl.ds(cs * NCAP + k, parts, stride=NCAP * cuts)
+
+
+def fill_container(out_ref, sel_ref, buf_ref, ent_ref, idx_ref, rnd):
+    cuts, slots, lanes = sel_ref.shape
+    picked = tn(one_hot_rows(ent_ref.shape[0], idx_ref[rnd : rnd + 1]), ent_ref[...])
+    for cs in range(cuts):
+        sel_ref[cs] = picked[:, cs * lanes : (cs + 1) * lanes]
+    for cs, rows, cells in container_cells(slots // NCAP, cuts):
+        buf_ref[cells, :] = sel_ref[cs, rows, :]
+    out_ref[...] = buf_ref[...].astype(BF)
 
 
 def round_kernel(in_ref, out_ref):
@@ -136,8 +132,8 @@
     out_ref.send()
 
 
-def serve_kernel(ent_ref, idx_ref, out_ref, sel_ref):
-    fill_container(out_ref, sel_ref, ent_ref, idx_ref, 0)
+def serve_kernel(ent_ref, idx_ref, out_ref, sel_ref, buf_ref):
+    fill_container(out_ref, sel_ref, buf_ref, ent_ref, idx_ref, 0)
 
 
 def tail_kernel(rnd, ent_ref, rel_ref, par_ref, head_ref, tail_ref, kind_ref, tq_ref, at_ref, n_ref, dtail_ref, pick_ref):
@@ -171,18 +167,13 @@
         dtail_ref[cut, :] = nn(at, tq_ref[...]).astype(BF)
 
 
-def neg_kernel(con_ref, tq_ref, n_ref, neg_ref, an_ref, dneg_ref):
+def neg_kernel(con_ref, tq_ref, n_ref, neg_ref, an_ref, dneg_ref, sel_ref, buf_ref):
     slots, width = neg_ref.shape
-    cuts = width // LANES
-    slot = iota((slots, con_ref.shape[0]), 0)
-    row = iota((slots, con_ref.shape[0]), 1) - ((slot // NCAP) * (NCAP * cuts) + slot % NCAP)
-
-    @pl.loop(0, cuts)
-    def _(cs):
-        perm = (row == cs * NCAP).astype(F32).astype(BF)
-        cut = pl.ds(pl.multiple_of(cs * LANES, LANES), LANES)
-        neg_ref[:, cut] = nn(perm, con_ref[...]).astype(BF)
-
+    buf_ref[...] = con_ref[...].astype(F32)
+    for cs, rows, cells in container_cells(slots // NCAP, width // LANES):
+        sel_ref[cs, rows, :] = buf_ref[cells, :]
+    for cs in range(width // LANES):
+        neg_ref[:, cs * LANES : (cs + 1) * LANES] = sel_ref[cs].astype(BF)
     wide = dneg_ref.shape[1]
     prob = jax.nn.sigmoid(nt(neg_ref[...], tq_ref[...]))
     an_ref[...] = (negative_weight * n_ref[:1] * prob).astype(BF)
@@ -216,27 +207,36 @@
             out_refs[s][rows:, :] = idx_ref[...]
 
 
-def rel_kernel(*refs):
-    given_ref, kept_ref, ents_ref = refs[2 * ROUNDS :]
-    rows, width = ents_ref.shape[1:]
-    for r in range(ROUNDS):
-        ents_ref[r] = refs[r].ready()[...].astype(BF)
-    g_refs = [ref.ready() for ref in refs[ROUNDS : 2 * ROUNDS]]
+def early_kernel(*refs):
+    out_ref = refs[-1]
+    count = len(refs) // 2
+    rows = refs[0].buffer.shape[0]
+    ents = [ref.ready()[...].astype(BF) for ref in refs[:count]]
+    gs = [ref.ready() for ref in refs[count:-1]]
+    kinds = gs[0].shape[0] // rows
+    pieces, _, line, width = out_ref.buffer.shape
+    for t in range(kinds):
+        total = sum(tn(ent, g[t * rows : (t + 1) * rows, :]) for ent, g in zip(ents, gs))
+        part = pieces // kinds
+        out_ref.buffer[t * part : (t + 1) * part] = total.reshape(part, 2, line, width)
+    out_ref.send()
+
+
+def rel_kernel(ent_ref, g_ref, early_ref, given_ref, kept_ref, full_ref):
+    rows = ent_ref.buffer.shape[0]
+    ent, g = ent_ref.ready(), g_ref.ready()
+    pieces, _, line, width = full_ref.shape
+    kinds = g.shape[0] // rows
+    part = pieces // kinds
+    early = None
+    for t in range(kinds):
+        total = tn(ent[...], g[t * rows : (t + 1) * rows, :]).reshape(part, 2, line, width)
+        early = early_ref.ready() if early is None else early
+        full_ref[t * part : (t + 1) * part] = total + early[t * part : (t + 1) * part]
     core = lax.rem(lax.axis_index("dom"), 2)
-    block = width // 4
-
-    def half(which, out_ref):
-        cut = pl.ds(pl.multiple_of(which * rows, rows), rows)
-
-        @pl.loop(0, 4)
-        def _(i):
-            part = pl.ds(pl.multiple_of(i * block, block), block)
-            total = sum(tn(ents_ref[r, :, part], g_refs[r][cut, :]) for r in range(ROUNDS))
-            out_ref[part, :] = total.astype(out_ref.dtype)
-
-    half(core, kept_ref.buffer)
+    given_ref[...] = full_ref[:, 1 - core].reshape(given_ref.shape).astype(BF)
+    kept_ref.buffer[...] = full_ref[:, core].reshape(given_ref.shape)
     kept_ref.send()
-    half(1 - core, given_ref)
 
 
 def pair_kernel(kept_ref, got_ref, out_ref):
@@ -286,13 +286,13 @@
     new_acc_ref[...] = jnp.broadcast_to(acc, (acc.shape[0], LANES)).T[:8]
 
 
-def update_kernel(rnd, grad_ref, ent_ref, acc_ref, idx_ref, new_acc_ref, bf_ref, con_ref, new_ref, keep_ref, sel_ref):
+def update_kernel(rnd, grad_ref, ent_ref, acc_ref, idx_ref, new_acc_ref, bf_ref, con_ref, new_ref, keep_ref, sel_ref, buf_ref):
     new_acc_ref[...] = update(grad_ref, ent_ref, acc_ref, new_ref.buffer)
     new_ref.send()
     bf_ref[...] = new_ref.buffer[...].astype(BF)
     keep_ref.buffer[...] = bf_ref[...]
     keep_ref.send()
-    fill_container(con_ref, sel_ref, bf_ref, idx_ref, rnd + 1)
+    fill_container(con_ref, sel_ref, buf_ref, bf_ref, idx_ref, rnd + 1)
 
 
 def total_kernel(parts_ref, out_ref):
@@ -320,9 +320,10 @@
 
     ent_bf = entities.astype(BF)
     accum = ent_accum.reshape(rows, 1)
-    chosen = pltpu.VMEM((slots, width), BF)
-    (con,) = call(serve_kernel, [((parts * cuts * NCAP, LANES), BF)], ent_bf, own, scratch=[chosen])
+    chosen = [pltpu.VMEM((cuts, slots, LANES), F32), pltpu.VMEM((parts * cuts * NCAP, LANES), F32)]
+    (con,) = call(serve_kernel, [((parts * cuts * NCAP, LANES), BF)], ent_bf, own, scratch=chosen)
     ents, gs = [entities], []
+    last_round = ROUNDS - 1
     (rel_bf,) = call(round_kernel, [(relations.shape, BF)], relations, late={0: kinds}, far=(0,))
     for rnd in range(ROUNDS):
         offset = rnd + 1
@@ -343,12 +344,22 @@
         )
         dtail = from_behind(dtail, "dom", offset)
         lines = 0 if rnd else INDEX_LINES
+        if last:
+            (early,) = call(
+                early_kernel,
+                [((parts, 2, kinds * width // (2 * parts), width), F32)],
+                *ents[:-1],
+                *gs,
+                late={i: rows if i < last_round else kinds * rows for i in range(2 * last_round)},
+                far=(0,),
+            )
         neg, an, dneg = call(
             neg_kernel,
             [((slots, width), BF), ((slots, kinds * rows), BF), ((reps * slots, wide), BF)],
             con,
             tq,
             n,
+            scratch=chosen,
         )
         dneg = all_ways(dneg.reshape(reps * parts, NCAP, wide), everyone).reshape(reps * slots, wide)
         *dhead, g = call(
@@ -407,27 +418,28 @@
                 own,
                 late={1: rows},
                 far=(3, 4),
-                scratch=[chosen],
+                scratch=chosen,
             )
             ents.append(keep)
     pair = [(i ^ 1, i) for i in range(parts)]
+    half = kinds * width // 2
+    piece = half // parts
     given, kept = call(
         rel_kernel,
-        [((width, width), BF), ((width, width), F32)],
-        *ents,
-        *gs,
-        late={i: rows if i < ROUNDS else kinds * rows for i in range(2 * ROUNDS)},
+        [((half, width), BF), ((half, width), F32)],
+        ents[-1],
+        gs[-1],
+        early,
+        late={0: rows, 1: kinds * rows, 2: parts},
         far=(1,),
-        scratch=[pltpu.VMEM((ROUNDS, rows, width), BF)],
+        scratch=[pltpu.VMEM((parts, 2, piece, width), F32)],
     )
     got = lax.ppermute(given, "dom", pair)
-    (drel,) = call(pair_kernel, [((width, width), BF)], kept, got, late={0: width})
-    piece = width // parts
+    (drel,) = call(pair_kernel, [((half, width), BF)], kept, got, late={0: half})
     drel = all_ways(drel.reshape(parts, piece, width), "dom")
-    (total,) = call(total_kernel, [((parts, kinds * piece, width), BF)], drel)
+    (total,) = call(total_kernel, [((parts, 2 * piece, width), BF)], drel)
     total = all_ways(total, "dom")
-    total = total.reshape(parts, kinds, piece, width).transpose(1, 0, 2, 3).reshape(kinds, width, width)
-    total = total.astype(F32)
+    total = lax.optimization_barrier(total.reshape(kinds, width, width)).astype(F32)
     new_rel_accum = rel_accum + total * total
     new_relations = relations - relation_rate * total * lax.rsqrt(new_rel_accum)
     return (entities, accum[0], new_relations, new_rel_accum)

time: 304 us -> 298 us (0.980)
    pallas_call x20 -> x21, Pallas kernels: 46.3 us -> 44.1 us  [call(): pl.pallas_call(body, out_shape=shapes, in_specs=[hbm if i in late else ne...]
  transfers between devices with their start and end apart: 28 -> 28, of which waited for: 19 -> 18; matrix products, arithmetic and copies ran while one was open for 1% -> 1% of each run, Pallas kernels for 8% -> 9%
where the time goes in v2:
time: 298 us; the launch traced here: 297 us
  starting transfers between devices  123 us (41%)
  waiting for transfers between devices  90.4 us (30%)
  Pallas kernels  44.1 us (15%)
  blocking collectives  30.2 us (10%)
  other arithmetic  5.46 us (2%)
    all_to_all x9, starting transfers between devices, all_ways(): return lax.all_to_all(block, axes, split_axis=0, concat_axis=0, tiled=True)  76.8 us
    ppermute x18, waiting for transfers between devices, from_behind(): lax.ppermute(block, axis, [((i - distance) % n, i) for i in range(n)])  59.3 us
    ppermute x18, starting transfers between devices, from_behind(): lax.ppermute(block, axis, [((i - distance) % n, i) for i in range(n)])  46.1 us
    pallas_call x21, Pallas kernels, call(): pl.pallas_call(body, out_shape=shapes, in_specs=[hbm if i in late else ne...  44.1 us
    all_to_all x2, blocking collectives, all_ways(): return lax.all_to_all(block, axes, split_axis=0, concat_axis=0, tiled=True)  30.2 us
    all_to_all x9, waiting for transfers between devices, all_ways(): return lax.all_to_all(block, axes, split_axis=0, concat_axis=0, tiled=True)  29.2 us
  transfers between devices with their start and end apart: 28, of which 18 were waited for; matrix products, arithmetic and copies ran while one was open for 1% of the time, Pallas kernels for 9%

profile of v2, /device:TPU:1, one launch (start us, length us, event | category | flops | bytes accessed | tf_op | source)
XLA Modules:
  0.0 297.0 jit_solution(14869227036353957002)
XLA Ops:
  2.3 10.3 %all-to-all-start = ((s32[64,1,12]{2,1,0:T(1,128)}), s32[64,1,12]{2,1,0:T(1,128)S(1)}, u32[]{:S(2)}, u32[]{:S(2)}) async-start(s32[64,1,12]{2,1,0:T(1,128)} %copy.17), calls=%async_computation | async-start | bytes 65536 | tf_op jit(solution)/shard_map/all_to_all | solution.py:106
  12.6 1.1 convert_element_type.7.refs_0_
  13.7 6.7 %all-to-all-done = s32[64,1,12]{2,1,0:T(1,128)S(1)} async-done(((s32[64,1,12]{2,1,0:T(1,128)}), s32[64,1,12]{2,1,0:T(1,128)S(1)}, u32[]{:S(2)}, u32[]{:S(2)}) %all-to-all-start) | async-done | bytes 3104 | tf_op jit(solution)/shard_map/all_to_all | solution.py:106
  20.7 1.1 shard_map.111
  21.8 4.7 %all-to-all-start.1 = ((bf16[64,16,128]{2,1,0:T(8,128)(2,1)}), bf16[64,16,128]{2,1,0:T(8,128)(2,1)S(1)}, u32[]{:S(2)}, u32[]{:S(2)}) async-start(bf16[64,16,128]{2,1,0:T(8,128)(2,1)} %bitcast.2), calls=%async_computation.1 | async-start | bytes 524288 | tf_op jit(solution)/shard_map/all_to_all | solution.py:106
  27.2 2.7 shard_map.112.refs_1_.refs_4_
  29.9 4.7 %collective-permute-done.refs_2_ = bf16[256,512]{1,0:T(8,128)(2,1)S(1)} collective-permute-done((bf16[256,512]{1,0:T(8,128)(2,1)S(1)}, bf16[256,512]{1,0:T(8,128)(2,1)S(1)}, u32[]{:S(2)}, u32[]{:S(2)}) %collective-permute-start) | collective-permute-done | bytes 262176 | tf_op jit(solution)/shard_map/ppermute | solution.py:111
  34.6 3.4 %shard_map.113 = (bf16[512,512]{1,0:T(8,128)(2,1)S(1)}, bf16[256,512]{1,0:T(8,128)(2,1)S(1)}, f32[8,512]{1,0:T(8,128)S(1)}, bf16[256,512]{1,0:T(8,128)(2,1)S(1)}) custom-call(bf16[256,512]{1,0:T(8,128)(2,1)S(1)} %convert_element_type.7.refs_0_, bf16[8,512,512]{2,1,0:T(8,128)(2,1)} %shard_map.112.refs_1_.refs_4_, ...), custom_call_target="tpu_custom_call" | custom-call | bytes 2665472 | tf_op jit(solution)/shard_map/pallas_call | solution.py:74
  38.0 1.4 shard_map.114
  39.4 15.2 %all-to-all-start.2 = ((bf16[256,4,128]{2,1,0:T(4,128)(2,1)}), bf16[256,4,128]{2,1,0:T(4,128)(2,1)S(1)}, u32[]{:S(2)}, u32[]{:S(2)}) async-start(bf16[256,4,128]{2,1,0:T(4,128)(2,1)} %bitcast.4), calls=%async_computation.2 | async-start | bytes 524288 | tf_op jit(solution)/shard_map/all_to_all | solution.py:106
  54.6 1.7 collective-permute-start.1
  56.6 4.6 %collective-permute-done.1.refs_5_ = bf16[256,512]{1,0:T(8,128)(2,1)S(1)} collective-permute-done((bf16[256,512]{1,0:T(8,128)(2,1)S(1)}, bf16[256,512]{1,0:T(8,128)(2,1)S(1)}, u32[]{:S(2)}, u32[]{:S(2)}) %collective-permute-start.1) | collective-permute-done | bytes 262176 | tf_op jit(solution)/shard_map/ppermute | solution.py:111
  61.2 2.6 shard_map.115
  63.7 2.1 collective-permute-start.2
  65.8 4.4 %collective-permute-start.3 = (bf16[272,128]{1,0:T(8,128)(2,1)S(1)}, bf16[272,128]{1,0:T(8,128)(2,1)S(1)}, u32[]{:S(2)}, u32[]{:S(2)}) collective-permute-start(bf16[272,128]{1,0:T(8,128)(2,1)S(1)} %get-tuple-element.63), channel_id=1, source_target_pairs={{2,0},{3,1},{0,2},{1,3},{6,4},{7,5},{4,6},{5,7},{10,8},{11,9},{8,1... | collective-permute-start | bytes 208904 | tf_op jit(solution)/shard_map/ppermute | solution.py:111
  70.2 2.5 collective-permute-start.4
  72.9 2.8 collective-permute-done.4.refs_4_.refs_8_
  75.7 1.0 shard_map.116
  76.7 4.3 %all-to-all-start.3 = ((bf16[4,256,128]{2,1,0:T(8,128)(2,1)}), bf16[4,256,128]{2,1,0:T(8,128)(2,1)S(1)}, u32[]{:S(2)}, u32[]{:S(2)}) async-start(bf16[4,256,128]{2,1,0:T(8,128)(2,1)} %shard_map.116), calls=%async_computation.3 | async-start | bytes 524288 | tf_op jit(solution)/shard_map/all_to_all | solution.py:106
  81.1 8.3 %all-to-all-done.3.refs_0_ = bf16[4,256,128]{2,1,0:T(8,128)(2,1)S(1)} async-done(((bf16[4,256,128]{2,1,0:T(8,128)(2,1)}), bf16[4,256,128]{2,1,0:T(8,128)(2,1)S(1)}, u32[]{:S(2)}, u32[]{:S(2)}) %all-to-all-start.3) | async-done | bytes 262176 | tf_op jit(solution)/shard_map/all_to_all | solution.py:106
  89.4 2.0 shard_map.117
  91.4 15.7 %all-to-all-start.4 = ((bf16[64,16,128]{2,1,0:T(8,128)(2,1)}), bf16[64,16,128]{2,1,0:T(8,128)(2,1)S(1)}, u32[]{:S(2)}, u32[]{:S(2)}) async-start(bf16[64,16,128]{2,1,0:T(8,128)(2,1)} %bitcast.7), calls=%async_computation.4 | async-start | bytes 524288 | tf_op jit(solution)/shard_map/all_to_all | solution.py:106
  107.2 6.3 %collective-permute-start.5 = (bf16[256,512]{1,0:T(8,128)(2,1)S(1)}, bf16[256,512]{1,0:T(8,128)(2,1)S(1)}, u32[]{:S(2)}, u32[]{:S(2)}) collective-permute-start(bf16[256,512]{1,0:T(8,128)(2,1)S(1)} %get-tuple-element.66.refs_0_), channel_id=1, source_target_pairs={{8,0},{12,4},{16,8},{20,12},{24,16},{28,20},{32,24},{36,28},{40,32... | collective-permute-start | bytes 786440 | tf_op jit(solution)/shard_map/ppermute | solution.py:111
  113.4 5.3 %collective-permute-done.5.refs_2_ = bf16[256,512]{1,0:T(8,128)(2,1)S(1)} collective-permute-done((bf16[256,512]{1,0:T(8,128)(2,1)S(1)}, bf16[256,512]{1,0:T(8,128)(2,1)S(1)}, u32[]{:S(2)}, u32[]{:S(2)}) %collective-permute-start.5) | collective-permute-done | bytes 262176 | tf_op jit(solution)/shard_map/ppermute | solution.py:111
  118.7 3.4 %shard_map.118 = (bf16[512,512]{1,0:T(8,128)(2,1)S(1)}, bf16[256,512]{1,0:T(8,128)(2,1)S(1)}, f32[8,512]{1,0:T(8,128)S(1)}, bf16[256,512]{1,0:T(8,128)(2,1)S(1)}) custom-call(bf16[256,512]{1,0:T(8,128)(2,1)S(1)} %get-tuple-element.66.refs_0_, bf16[8,512,512]{2,1,0:T(8,128)(2,1)} %shard_map.112.refs_1_.refs_4_, ...), custom_call_target="tpu_custom_call" | custom-call | bytes 2665472 | tf_op jit(solution)/shard_map/pallas_call | solution.py:74
  122.1 1.4 shard_map.119
  123.5 9.8 %all-to-all-start.5 = ((bf16[256,4,128]{2,1,0:T(4,128)(2,1)}), bf16[256,4,128]{2,1,0:T(4,128)(2,1)S(1)}, u32[]{:S(2)}, u32[]{:S(2)}) async-start(bf16[256,4,128]{2,1,0:T(4,128)(2,1)} %bitcast.9), calls=%async_computation.5 | async-start | bytes 524288 | tf_op jit(solution)/shard_map/all_to_all | solution.py:106
  133.3 1.4 collective-permute-start.6
  134.8 15.6 %collective-permute-done.6.refs_5_ = bf16[256,512]{1,0:T(8,128)(2,1)S(1)} collective-permute-done((bf16[256,512]{1,0:T(8,128)(2,1)S(1)}, bf16[256,512]{1,0:T(8,128)(2,1)S(1)}, u32[]{:S(2)}, u32[]{:S(2)}) %collective-permute-start.6) | collective-permute-done | bytes 262176 | tf_op jit(solution)/shard_map/ppermute | solution.py:111
  150.4 2.5 shard_map.120
  153.0 2.0 collective-permute-start.7
  155.0 2.9 collective-permute-start.8
  157.9 3.3 %collective-permute-start.9 = (bf16[256,128]{1,0:T(8,128)(2,1)S(1)}, bf16[256,128]{1,0:T(8,128)(2,1)S(1)}, u32[]{:S(2)}, u32[]{:S(2)}) collective-permute-start(bf16[256,128]{1,0:T(8,128)(2,1)S(1)} %get-tuple-element.77), channel_id=1, source_target_pairs={{1,0},{2,1},{3,2},{0,3},{5,4},{6,5},{7,6},{4,7},{9,8},{10,9},{11,1... | collective-permute-start | bytes 196616 | tf_op jit(solution)/shard_map/ppermute | solution.py:111
  161.2 1.2 collective-permute-done.8.refs_3_
  162.4 1.8 collective-permute-done.9.refs_4_
  164.4 13.7 %all_to_all.59.refs_0_ = bf16[4,256,128]{2,1,0:T(8,128)(2,1)S(1)} all-to-all(bf16[4,256,128]{2,1,0:T(8,128)(2,1)S(1)} %shard_map.121), channel_id=1, replica_groups=mesh['dom'=64,'rep'=4] {'rep'}, dimensions={0} | all-to-all | bytes 524288 | tf_op jit(solution)/shard_map/all_to_all | solution.py:106
  178.2 3.0 shard_map.122
  181.2 3.1 %collective-permute-start.10 = (bf16[256,512]{1,0:T(8,128)(2,1)S(1)}, bf16[256,512]{1,0:T(8,128)(2,1)S(1)}, u32[]{:S(2)}, u32[]{:S(2)}) collective-permute-start(bf16[256,512]{1,0:T(8,128)(2,1)S(1)} %get-tuple-element.81.refs_0_), channel_id=1, source_target_pairs={{12,0},{16,4},{20,8},{24,12},{28,16},{32,20},{36,24},{40,28},{44,3... | collective-permute-start | bytes 786440 | tf_op jit(solution)/shard_map/ppermute | solution.py:111
  184.3 5.5 %all-to-all-start.7 = ((bf16[64,16,128]{2,1,0:T(8,128)(2,1)}), bf16[64,16,128]{2,1,0:T(8,128)(2,1)S(1)}, u32[]{:S(2)}, u32[]{:S(2)}) async-start(bf16[64,16,128]{2,1,0:T(8,128)(2,1)} %bitcast.11), calls=%async_computation.7 | async-start | bytes 524288 | tf_op jit(solution)/shard_map/all_to_all | solution.py:106
  190.4 3.4 %shard_map.123 = (bf16[512,512]{1,0:T(8,128)(2,1)S(1)}, bf16[256,512]{1,0:T(8,128)(2,1)S(1)}, f32[8,512]{1,0:T(8,128)S(1)}, bf16[256,512]{1,0:T(8,128)(2,1)S(1)}) custom-call(bf16[256,512]{1,0:T(8,128)(2,1)S(1)} %get-tuple-element.81.refs_0_, bf16[8,512,512]{2,1,0:T(8,128)(2,1)} %shard_map.112.refs_1_.refs_4_, ...), custom_call_target="tpu_custom_call" | custom-call | bytes 2665472 | tf_op jit(solution)/shard_map/pallas_call | solution.py:74
  193.8 2.9 collective-permute-start.11
  196.7 3.4 %shard_map.128.refs_2_ = f32[128,2,8,512]{3,2,1,0:T(8,128)} custom-call(f32[256,512]{1,0:T(8,128)S(1)} %copy-done, bf16[4096,512]{1,0:T(8,128)(2,1)} %get-tuple-element.99.refs_1_, bf16[4096,512]{1,0:T(8,128)(2,1)} %get-tuple-element.100.refs_2_, bf16[4096,512]{1,0:T(8,128)(2,1)} %get-tuple-element.101.refs_3_), custom_call_target="tpu_custom_call" | custom-call | bytes 3932160 | tf_op jit(solution)/shard_map/pallas_call | solution.py:74
  200.1 1.4 shard_map.124
  201.6 5.6 %collective-permute-done.11.refs_5_ = bf16[256,512]{1,0:T(8,128)(2,1)S(1)} collective-permute-done((bf16[256,512]{1,0:T(8,128)(2,1)S(1)}, bf16[256,512]{1,0:T(8,128)(2,1)S(1)}, u32[]{:S(2)}, u32[]{:S(2)}) %collective-permute-start.11) | collective-permute-done | bytes 262176 | tf_op jit(solution)/shard_map/ppermute | solution.py:111
  207.1 2.5 shard_map.125
  209.7 3.5 %shard_map.129 = (bf16[512,512]{1,0:T(8,128)(2,1)S(1)}, f32[2048,512]{1,0:T(8,128)}) custom-call(bf16[4096,512]{1,0:T(8,128)(2,1)} %get-tuple-element.97.refs_0_, bf16[4096,512]{1,0:T(8,128)(2,1)} %get-tuple-element.98.refs_1_, f32[128,2,8,512]{3,2,1,0:T(8,128)} %shard_map.128.refs_2_), custom_call_target="tpu_custom_call" | custom-call | bytes 4456448 | tf_op jit(solution)/shard_map/pallas_call | solution.py:74
  213.3 1.9 collective-permute-done.18.refs_1_
  215.2 1.4 shard_map.130
  216.6 16.5 %all_to_all.60.refs_0_ = bf16[64,8,512]{2,1,0:T(8,128)(2,1)S(1)} all-to-all(bf16[64,8,512]{2,1,0:T(8,128)(2,1)S(1)} %bitcast.24), channel_id=1, replica_groups=mesh['dom'=64,'rep'=4] {'dom'}, dimensions={0} | all-to-all | bytes 1048576 | tf_op jit(solution)/shard_map/all_to_all | solution.py:106
  233.1 6.0 %all-to-all-start.8 = ((bf16[256,4,128]{2,1,0:T(4,128)(2,1)}), bf16[256,4,128]{2,1,0:T(4,128)(2,1)S(1)}, u32[]{:S(2)}, u32[]{:S(2)}) async-start(bf16[256,4,128]{2,1,0:T(4,128)(2,1)} %bitcast.13), calls=%async_computation.8 | async-start | bytes 524288 | tf_op jit(solution)/shard_map/all_to_all | solution.py:106
  239.0 1.1 shard_map.131
  240.2 14.3 %all-to-all-done.8 = bf16[256,4,128]{2,1,0:T(4,128)(2,1)S(1)} async-done(((bf16[256,4,128]{2,1,0:T(4,128)(2,1)}), bf16[256,4,128]{2,1,0:T(4,128)(2,1)S(1)}, u32[]{:S(2)}, u32[]{:S(2)}) %all-to-all-start.8) | async-done | bytes 262176 | tf_op jit(solution)/shard_map/all_to_all | solution.py:106
  254.5 5.2 %all-to-all-start.10 = ((bf16[64,16,512]{2,1,0:T(8,128)(2,1)}), bf16[64,16,512]{2,1,0:T(8,128)(2,1)S(1)}, u32[]{:S(2)}, u32[]{:S(2)}) async-start(bf16[64,16,512]{2,1,0:T(8,128)(2,1)} %shard_map.131), calls=%async_computation.10 | async-start | bytes 2097152 | tf_op jit(solution)/shard_map/all_to_all | solution.py:106
  260.0 2.4 collective-permute-start.13
  262.4 1.3 collective-permute-start.14
  263.7 11.3 %collective-permute-done.12.refs_2_ = bf16[256,128]{1,0:T(8,128)(2,1)S(1)} collective-permute-done((bf16[256,128]{1,0:T(8,128)(2,1)S(1)}, bf16[256,128]{1,0:T(8,128)(2,1)S(1)}, u32[]{:S(2)}, u32[]{:S(2)}) %collective-permute-start.12) | collective-permute-done | bytes 65568 | tf_op jit(solution)/shard_map/ppermute | solution.py:111
  275.0 1.0 collective-permute-done.13.refs_3_
  276.4 3.7 %collective-permute-start.17 = (bf16[256,128]{1,0:T(8,128)(2,1)S(1)}, bf16[256,128]{1,0:T(8,128)(2,1)S(1)}, u32[]{:S(2)}, u32[]{:S(2)}) collective-permute-start(bf16[256,128]{1,0:T(8,128)(2,1)S(1)} %bitcast.31), channel_id=1, source_target_pairs={{3,0},{0,1},{1,2},{2,3},{7,4},{4,5},{5,6},{6,7},{11,8},{8,9},{9,10... | collective-permute-start | bytes 196616 | tf_op jit(solution)/shard_map/ppermute | solution.py:111
  280.1 1.7 collective-permute-start.16
  281.8 3.5 %collective-permute-start.15 = (bf16[256,128]{1,0:T(8,128)(2,1)S(1)}, bf16[256,128]{1,0:T(8,128)(2,1)S(1)}, u32[]{:S(2)}, u32[]{:S(2)}) collective-permute-start(bf16[256,128]{1,0:T(8,128)(2,1)S(1)} %bitcast.33), channel_id=1, source_target_pairs={{1,0},{2,1},{3,2},{0,3},{5,4},{6,5},{7,6},{4,7},{9,8},{10,9},{11,1... | collective-permute-start | bytes 196616 | tf_op jit(solution)/shard_map/ppermute | solution.py:111
  285.3 2.2 collective-permute-done.16.refs_2_
  287.5 2.5 collective-permute-done.15.refs_1_
  290.0 2.1 shard_map.127
  292.7 4.4 %fusion.1 = (f32[2,512,512]{2,1,0:T(8,128)}, f32[2,512,512]{2,1,0:T(8,128)}) fusion(f32[2,512,512]{2,1,0:T(8,128)S(1)} %copy-done.4, bf16[2,512,512]{2,1,0:T(8,128)(2,1)S(1)} %bitcast.35, f32[2,512,512]{2,1,0:T(8,128)} %param.11), kind=kLoop, calls=%fused_computation.3 | loop fusion | flops 3145728 | bytes 9437184 | tf_op jit(solution)/shard_map/sub | solution.py:444
  (47 shorter events, 5.3 us)
Async XLA Ops:
  2.3 18.1 %all-to-all-start = ((s32[64,1,12]{2,1,0:T(1,128)}), s32[64,1,12]{2,1,0:T(1,128)S(1)}, u32[]{:S(2)}, u32[]{:S(2)}) async-start(s32[64,1,12]{2,1,0:T(1,128)} %copy.17), calls=%async_computation | async-start | bytes 65536 | tf_op jit(solution)/shard_map/all_to_all | solution.py:106
  21.8 16.2 %all-to-all-start.1 = ((bf16[64,16,128]{2,1,0:T(8,128)(2,1)}), bf16[64,16,128]{2,1,0:T(8,128)(2,1)S(1)}, u32[]{:S(2)}, u32[]{:S(2)}) async-start(bf16[64,16,128]{2,1,0:T(8,128)(2,1)} %bitcast.2), calls=%async_computation.1 | async-start | bytes 524288 | tf_op jit(solution)/shard_map/all_to_all | solution.py:106
  26.5 8.1 %copy-start.1 = (s32[3,768]{1,0:T(4,128)S(1)}, s32[3,768]{1,0:T(4,128)}, u32[]{:S(2)}) copy-start(s32[3,768]{1,0:T(4,128)} %refs_3_.5) | copy-start | bytes 27652
  26.5 8.1 %copy-start.2 = (s32[3,768]{1,0:T(4,128)S(1)}, s32[3,768]{1,0:T(4,128)}, u32[]{:S(2)}) copy-start(s32[3,768]{1,0:T(4,128)} %refs_4_.5) | copy-start | bytes 27652
  26.5 8.1 %copy-start.3 = (s32[3,768]{1,0:T(4,128)S(1)}, s32[3,768]{1,0:T(4,128)}, u32[]{:S(2)}) copy-start(s32[3,768]{1,0:T(4,128)} %refs_5_.5) | copy-start | bytes 27652
  26.5 8.0 %collective-permute-start = (bf16[256,512]{1,0:T(8,128)(2,1)S(1)}, bf16[256,512]{1,0:T(8,128)(2,1)S(1)}, u32[]{:S(2)}, u32[]{:S(2)}) collective-permute-start(bf16[256,512]{1,0:T(8,128)(2,1)S(1)} %convert_element_type.7.refs_0_), channel_id=1, source_target_pairs={{4,0},{8,4},{12,8},{16,12},{20,16},{24,20},{28,24},{32,28},{36,32}... | collective-permute-start | bytes 786440 | tf_op jit(solution)/shard_map/ppermute | solution.py:111
  39.4 36.3 %all-to-all-start.2 = ((bf16[256,4,128]{2,1,0:T(4,128)(2,1)}), bf16[256,4,128]{2,1,0:T(4,128)(2,1)S(1)}, u32[]{:S(2)}, u32[]{:S(2)}) async-start(bf16[256,4,128]{2,1,0:T(4,128)(2,1)} %bitcast.4), calls=%async_computation.2 | async-start | bytes 524288 | tf_op jit(solution)/shard_map/all_to_all | solution.py:106
  54.6 6.6 %collective-permute-start.1 = (bf16[256,512]{1,0:T(8,128)(2,1)S(1)}, bf16[256,512]{1,0:T(8,128)(2,1)S(1)}, u32[]{:S(2)}, u32[]{:S(2)}) collective-permute-start(bf16[256,512]{1,0:T(8,128)(2,1)S(1)} %get-tuple-element.60), channel_id=1, source_target_pairs={{252,0},{0,4},{4,8},{8,12},{12,16},{16,20},{20,24},{24,28},{28,32}... | collective-permute-start | bytes 786440 | tf_op jit(solution)/shard_map/ppermute | solution.py:111
  61.2 19.8 %copy-start.5 = (f32[256]{0:T(256)S(1)}, f32[256]{0:T(256)}, u32[]{:S(2)}) copy-start(f32[256]{0:T(256)} %param.9) | copy-start | bytes 3076
  63.7 25.6 %copy-start = (f32[256,512]{1,0:T(8,128)S(1)}, f32[256,512]{1,0:T(8,128)}, u32[]{:S(2)}) copy-start(f32[256,512]{1,0:T(8,128)} %refs_0_.3) | copy-start | bytes 1572868
  63.7 8.9 %collective-permute-start.2 = (bf16[272,128]{1,0:T(8,128)(2,1)S(1)}, bf16[272,128]{1,0:T(8,128)(2,1)S(1)}, u32[]{:S(2)}, u32[]{:S(2)}) collective-permute-start(bf16[272,128]{1,0:T(8,128)(2,1)S(1)} %get-tuple-element.62), channel_id=1, source_target_pairs={{3,0},{0,1},{1,2},{2,3},{7,4},{4,5},{5,6},{6,7},{11,8},{8,9},{9,10... | collective-permute-start | bytes 208904 | tf_op jit(solution)/shard_map/ppermute | solution.py:111
  65.8 7.1 %collective-permute-start.3 = (bf16[272,128]{1,0:T(8,128)(2,1)S(1)}, bf16[272,128]{1,0:T(8,128)(2,1)S(1)}, u32[]{:S(2)}, u32[]{:S(2)}) collective-permute-start(bf16[272,128]{1,0:T(8,128)(2,1)S(1)} %get-tuple-element.63), channel_id=1, source_target_pairs={{2,0},{3,1},{0,2},{1,3},{6,4},{7,5},{4,6},{5,7},{10,8},{11,9},{8,1... | collective-permute-start | bytes 208904 | tf_op jit(solution)/shard_map/ppermute | solution.py:111
  70.2 5.5 %collective-permute-start.4 = (bf16[272,128]{1,0:T(8,128)(2,1)S(1)}, bf16[272,128]{1,0:T(8,128)(2,1)S(1)}, u32[]{:S(2)}, u32[]{:S(2)}) collective-permute-start(bf16[272,128]{1,0:T(8,128)(2,1)S(1)} %get-tuple-element.64), channel_id=1, source_target_pairs={{1,0},{2,1},{3,2},{0,3},{5,4},{6,5},{7,6},{4,7},{9,8},{10,9},{11,1... | collective-permute-start | bytes 208904 | tf_op jit(solution)/shard_map/ppermute | solution.py:111
  76.7 12.7 %all-to-all-start.3 = ((bf16[4,256,128]{2,1,0:T(8,128)(2,1)}), bf16[4,256,128]{2,1,0:T(8,128)(2,1)S(1)}, u32[]{:S(2)}, u32[]{:S(2)}) async-start(bf16[4,256,128]{2,1,0:T(8,128)(2,1)} %shard_map.116), calls=%async_computation.3 | async-start | bytes 524288 | tf_op jit(solution)/shard_map/all_to_all | solution.py:106
  91.4 30.7 %all-to-all-start.4 = ((bf16[64,16,128]{2,1,0:T(8,128)(2,1)}), bf16[64,16,128]{2,1,0:T(8,128)(2,1)S(1)}, u32[]{:S(2)}, u32[]{:S(2)}) async-start(bf16[64,16,128]{2,1,0:T(8,128)(2,1)} %bitcast.7), calls=%async_computation.4 | async-start | bytes 524288 | tf_op jit(solution)/shard_map/all_to_all | solution.py:106
  107.2 11.5 %collective-permute-start.5 = (bf16[256,512]{1,0:T(8,128)(2,1)S(1)}, bf16[256,512]{1,0:T(8,128)(2,1)S(1)}, u32[]{:S(2)}, u32[]{:S(2)}) collective-permute-start(bf16[256,512]{1,0:T(8,128)(2,1)S(1)} %get-tuple-element.66.refs_0_), channel_id=1, source_target_pairs={{8,0},{12,4},{16,8},{20,12},{24,16},{28,20},{32,24},{36,28},{40,32... | collective-permute-start | bytes 786440 | tf_op jit(solution)/shard_map/ppermute | solution.py:111
  123.5 40.6 %all-to-all-start.5 = ((bf16[256,4,128]{2,1,0:T(4,128)(2,1)}), bf16[256,4,128]{2,1,0:T(4,128)(2,1)S(1)}, u32[]{:S(2)}, u32[]{:S(2)}) async-start(bf16[256,4,128]{2,1,0:T(4,128)(2,1)} %bitcast.9), calls=%async_computation.5 | async-start | bytes 524288 | tf_op jit(solution)/shard_map/all_to_all | solution.py:106
  133.3 17.1 %collective-permute-start.6 = (bf16[256,512]{1,0:T(8,128)(2,1)S(1)}, bf16[256,512]{1,0:T(8,128)(2,1)S(1)}, u32[]{:S(2)}, u32[]{:S(2)}) collective-permute-start(bf16[256,512]{1,0:T(8,128)(2,1)S(1)} %get-tuple-element.73), channel_id=1, source_target_pairs={{248,0},{252,4},{0,8},{4,12},{8,16},{12,20},{16,24},{20,28},{24,32... | collective-permute-start | bytes 786440 | tf_op jit(solution)/shard_map/ppermute | solution.py:111
  153.0 8.2 %collective-permute-start.7 = (bf16[256,128]{1,0:T(8,128)(2,1)S(1)}, bf16[256,128]{1,0:T(8,128)(2,1)S(1)}, u32[]{:S(2)}, u32[]{:S(2)}) collective-permute-start(bf16[256,128]{1,0:T(8,128)(2,1)S(1)} %get-tuple-element.75), channel_id=1, source_target_pairs={{3,0},{0,1},{1,2},{2,3},{7,4},{4,5},{5,6},{6,7},{11,8},{8,9},{9,10... | collective-permute-start | bytes 196616 | tf_op jit(solution)/shard_map/ppermute | solution.py:111
  155.0 7.4 %collective-permute-start.8 = (bf16[256,128]{1,0:T(8,128)(2,1)S(1)}, bf16[256,128]{1,0:T(8,128)(2,1)S(1)}, u32[]{:S(2)}, u32[]{:S(2)}) collective-permute-start(bf16[256,128]{1,0:T(8,128)(2,1)S(1)} %get-tuple-element.76), channel_id=1, source_target_pairs={{2,0},{3,1},{0,2},{1,3},{6,4},{7,5},{4,6},{5,7},{10,8},{11,9},{8,1... | collective-permute-start | bytes 196616 | tf_op jit(solution)/shard_map/ppermute | solution.py:111
  157.9 6.3 %collective-permute-start.9 = (bf16[256,128]{1,0:T(8,128)(2,1)S(1)}, bf16[256,128]{1,0:T(8,128)(2,1)S(1)}, u32[]{:S(2)}, u32[]{:S(2)}) collective-permute-start(bf16[256,128]{1,0:T(8,128)(2,1)S(1)} %get-tuple-element.77), channel_id=1, source_target_pairs={{1,0},{2,1},{3,2},{0,3},{5,4},{6,5},{7,6},{4,7},{9,8},{10,9},{11,1... | collective-permute-start | bytes 196616 | tf_op jit(solution)/shard_map/ppermute | solution.py:111
  181.2 9.3 %collective-permute-start.10 = (bf16[256,512]{1,0:T(8,128)(2,1)S(1)}, bf16[256,512]{1,0:T(8,128)(2,1)S(1)}, u32[]{:S(2)}, u32[]{:S(2)}) collective-permute-start(bf16[256,512]{1,0:T(8,128)(2,1)S(1)} %get-tuple-element.81.refs_0_), channel_id=1, source_target_pairs={{12,0},{16,4},{20,8},{24,12},{28,16},{32,20},{36,24},{40,28},{44,3... | collective-permute-start | bytes 786440 | tf_op jit(solution)/shard_map/ppermute | solution.py:111
  184.3 15.8 %all-to-all-start.7 = ((bf16[64,16,128]{2,1,0:T(8,128)(2,1)}), bf16[64,16,128]{2,1,0:T(8,128)(2,1)S(1)}, u32[]{:S(2)}, u32[]{:S(2)}) async-start(bf16[64,16,128]{2,1,0:T(8,128)(2,1)} %bitcast.11), calls=%async_computation.7 | async-start | bytes 524288 | tf_op jit(solution)/shard_map/all_to_all | solution.py:106
  193.8 13.3 %collective-permute-start.11 = (bf16[256,512]{1,0:T(8,128)(2,1)S(1)}, bf16[256,512]{1,0:T(8,128)(2,1)S(1)}, u32[]{:S(2)}, u32[]{:S(2)}) collective-permute-start(bf16[256,512]{1,0:T(8,128)(2,1)S(1)} %get-tuple-element.88), channel_id=1, source_target_pairs={{244,0},{248,4},{252,8},{0,12},{4,16},{8,20},{12,24},{16,28},{20,3... | collective-permute-start | bytes 786440 | tf_op jit(solution)/shard_map/ppermute | solution.py:111
  213.2 2.0 collective-permute-start.18
  233.1 21.4 %all-to-all-start.8 = ((bf16[256,4,128]{2,1,0:T(4,128)(2,1)}), bf16[256,4,128]{2,1,0:T(4,128)(2,1)S(1)}, u32[]{:S(2)}, u32[]{:S(2)}) async-start(bf16[256,4,128]{2,1,0:T(4,128)(2,1)} %bitcast.13), calls=%async_computation.8 | async-start | bytes 524288 | tf_op jit(solution)/shard_map/all_to_all | solution.py:106
  254.5 38.2 %all-to-all-start.10 = ((bf16[64,16,512]{2,1,0:T(8,128)(2,1)}), bf16[64,16,512]{2,1,0:T(8,128)(2,1)S(1)}, u32[]{:S(2)}, u32[]{:S(2)}) async-start(bf16[64,16,512]{2,1,0:T(8,128)(2,1)} %shard_map.131), calls=%async_computation.10 | async-start | bytes 2097152 | tf_op jit(solution)/shard_map/all_to_all | solution.py:106
  259.7 15.3 %collective-permute-start.12 = (bf16[256,128]{1,0:T(8,128)(2,1)S(1)}, bf16[256,128]{1,0:T(8,128)(2,1)S(1)}, u32[]{:S(2)}, u32[]{:S(2)}) collective-permute-start(bf16[256,128]{1,0:T(8,128)(2,1)S(1)} %get-tuple-element.90), channel_id=1, source_target_pairs={{3,0},{0,1},{1,2},{2,3},{7,4},{4,5},{5,6},{6,7},{11,8},{8,9},{9,10... | collective-permute-start | bytes 196616 | tf_op jit(solution)/shard_map/ppermute | solution.py:111
  260.0 16.1 %collective-permute-start.13 = (bf16[256,128]{1,0:T(8,128)(2,1)S(1)}, bf16[256,128]{1,0:T(8,128)(2,1)S(1)}, u32[]{:S(2)}, u32[]{:S(2)}) collective-permute-start(bf16[256,128]{1,0:T(8,128)(2,1)S(1)} %get-tuple-element.91), channel_id=1, source_target_pairs={{2,0},{3,1},{0,2},{1,3},{6,4},{7,5},{4,6},{5,7},{10,8},{11,9},{8,1... | collective-permute-start | bytes 196616 | tf_op jit(solution)/shard_map/ppermute | solution.py:111
  262.4 13.7 %collective-permute-start.14 = (bf16[256,128]{1,0:T(8,128)(2,1)S(1)}, bf16[256,128]{1,0:T(8,128)(2,1)S(1)}, u32[]{:S(2)}, u32[]{:S(2)}) collective-permute-start(bf16[256,128]{1,0:T(8,128)(2,1)S(1)} %get-tuple-element.92), channel_id=1, source_target_pairs={{1,0},{2,1},{3,2},{0,3},{5,4},{6,5},{7,6},{4,7},{9,8},{10,9},{11,1... | collective-permute-start | bytes 196616 | tf_op jit(solution)/shard_map/ppermute | solution.py:111
  276.4 9.0 %collective-permute-start.17 = (bf16[256,128]{1,0:T(8,128)(2,1)S(1)}, bf16[256,128]{1,0:T(8,128)(2,1)S(1)}, u32[]{:S(2)}, u32[]{:S(2)}) collective-permute-start(bf16[256,128]{1,0:T(8,128)(2,1)S(1)} %bitcast.31), channel_id=1, source_target_pairs={{3,0},{0,1},{1,2},{2,3},{7,4},{4,5},{5,6},{6,7},{11,8},{8,9},{9,10... | collective-permute-start | bytes 196616 | tf_op jit(solution)/shard_map/ppermute | solution.py:111
  280.1 7.4 %collective-permute-start.16 = (bf16[256,128]{1,0:T(8,128)(2,1)S(1)}, bf16[256,128]{1,0:T(8,128)(2,1)S(1)}, u32[]{:S(2)}, u32[]{:S(2)}) collective-permute-start(bf16[256,128]{1,0:T(8,128)(2,1)S(1)} %bitcast.32), channel_id=1, source_target_pairs={{2,0},{3,1},{0,2},{1,3},{6,4},{7,5},{4,6},{5,7},{10,8},{11,9},{8,1... | collective-permute-start | bytes 196616 | tf_op jit(solution)/shard_map/ppermute | solution.py:111
  281.8 8.1 %collective-permute-start.15 = (bf16[256,128]{1,0:T(8,128)(2,1)S(1)}, bf16[256,128]{1,0:T(8,128)(2,1)S(1)}, u32[]{:S(2)}, u32[]{:S(2)}) collective-permute-start(bf16[256,128]{1,0:T(8,128)(2,1)S(1)} %bitcast.33), channel_id=1, source_target_pairs={{1,0},{2,1},{3,2},{0,3},{5,4},{6,5},{7,6},{4,7},{9,8},{10,9},{11,1... | collective-permute-start | bytes 196616 | tf_op jit(solution)/shard_map/ppermute | solution.py:111
  290.0 2.7 copy-start.4
